TPU v7x, 256 devices: a whole 4x4x8 slice. The times are simulated.
256 devices in a mesh: seq: 16 (over y, z_hi, core), mp: 16 (over z_lo, x).
Axes of the slice: x: 4, y: 4, z: 8 (z_hi: 2, z_lo: 4; z = z_hi * 4 + z_lo), core: 2. Of those that a mesh axis runs over, the one named last changes fastest.
Arguments:
- hidden_in: bfloat16 [2048, 2048], P('seq'), may hold values from -0.59765625 to 0.59765625
- input_gain: float32 [2048], replicated, may hold values from 0.25 to 1.75
- w_query: bfloat16 [2048, 2048], P(None, 'mp'), may hold values from -0.125 to 0.125
- key_value_weight: bfloat16 [2048, 4096], P(None, 'mp'), may hold values from -1 to 1, as said below
- query_gain: float32 [128], replicated, may hold values from 0.25 to 1.75
- key_gain: float32 [128], replicated, may hold values from 0.25 to 1.75
- w_out: bfloat16 [2048, 2048], P('mp'), may hold values from -0.125 to 0.125
- post_gain: float32 [2048], replicated, may hold values from 0.25 to 1.75
- w_gate: bfloat16 [2048, 6144], P(None, 'mp'), may hold values from -0.125 to 0.125
- w_up: bfloat16 [2048, 6144], P(None, 'mp'), may hold values from -0.125 to 0.125
- w_down: bfloat16 [6144, 2048], P('mp'), may hold values from -0.078125 to 0.078125
- prefix_slot_cache: bfloat16 [32, 256, 8, 256], P('seq'), may hold values from -240 to 240, as said below
- block_table: int32 [32], replicated, may hold values from 0 to 31, each once
- request_prefix: int32 [32], replicated, may hold values from 0 to 3
- suffix_lengths: int32 [32], replicated, may hold values from 1 to 256, 2048 in all
Outputs:
- hidden_out: bfloat16 [2048, 2048], P('seq', 'mp')
- suffix_key_values: bfloat16 [2048, 2048], P('seq', 'mp')
Inputs may be any that keep to these rules, and one draw needn't show every extreme that they name: block_table[p * 8 + i] is the slot holding block i of prefix p; every slot appears once. `suffix_lengths`: the lengths add up to 2048 and the longest is exactly 256. `prefix_slot_cache`: per slot, position and key-value head: a key in the first 128 entries, a value in the last 128. `key_value_weight`: columns of key-value head k: 2 equal blocks of 256, starting at k * 2 * 2 * 128.
All inputs are finite; a program needn't handle non-finite values.
Results may differ from a plain program's by a relative error of at most 0.025.
The roundings to bfloat16 on the way count: a program that leaves them out, or rounds other values in their place, can miss the bound.
Values may be sent and summed in bfloat16 or wider, within the bound.
A program may use at most 64 MiB of HBM per device.

v0:
```python
import math

import jax
import jax.numpy as jnp
from jax import lax
from jax.sharding import PartitionSpec as P

QUERY_HEADS = 16
KEY_VALUE_HEADS = 8
HEAD_WIDTH = 128
N_PREFIX = 4


EPSILON = 1e-06
THETA = 1000000.0
NEGATIVE_FLOOR = -1e30


def token_tables(request_prefix, suffix_lengths, positions, prefix_length):
    request_ends = jnp.cumsum(suffix_lengths)
    starts = request_ends - suffix_lengths
    inside = (
        (positions[:, None] >= starts[None, :]) & (positions[:, None] < request_ends[None, :])
    ).astype(jnp.int32)
    request_ids = jnp.arange(suffix_lengths.shape[0], dtype=jnp.int32)
    request_of = jnp.sum(inside * request_ids[None, :], axis=1)
    start_of = jnp.sum(inside * starts[None, :], axis=1)
    prefix_of = jnp.sum(inside * request_prefix[None, :], axis=1)
    rotary_pos = prefix_length + positions - start_of
    return (request_of, prefix_of, rotary_pos)


def row_norm(values, gain):
    return values * lax.rsqrt(jnp.mean(values * values, axis=-1, keepdims=True) + EPSILON) * gain


def head_norm(values, gain):
    return values * lax.rsqrt(jnp.mean(values * values, axis=-1, keepdims=True) + EPSILON) * gain


def rotate(values, rotary_pos):
    half_dim = values.shape[-1] // 2
    freq_ids = jnp.arange(half_dim).astype(jnp.float32)
    inverse = jnp.exp(freq_ids * (-2.0 * math.log(THETA) / values.shape[-1]))
    angles = rotary_pos.astype(jnp.float32)[:, None] * inverse[None, :]
    cosine = jnp.cos(angles)[:, None, :]
    sine_part = jnp.sin(angles)[:, None, :]
    first_half = values[..., :half_dim]
    second_half = values[..., half_dim:]
    return jnp.concatenate(
        [
            first_half * cosine - second_half * sine_part,
            second_half * cosine + first_half * sine_part,
        ],
        axis=-1,
    )


def allowed_keys(query_req, query_pre, query_pos, key_pre, key_req, key_pos):
    same_prefix = key_pre[None, :] == query_pre[:, None]
    same_request = (key_req[None, :] == query_req[:, None]) & (
        key_pos[None, :] <= query_pos[:, None]
    )
    return same_prefix | same_request


def group_partial(query_rows_all, allowed, key_row_block, value_row_block):
    scaling = 1.0 / math.sqrt(query_rows_all.shape[-1])
    scores = (
        jnp.einsum(
            "nkgd,mkd->nkgm", query_rows_all, key_row_block, preferred_element_type=jnp.float32
        )
        * scaling
    )
    allowed_full = allowed[:, None, None, :]
    scores = jnp.where(allowed_full, scores, NEGATIVE_FLOOR)
    highest_score = jnp.max(scores, axis=-1)
    weights = jnp.where(allowed_full, jnp.exp(scores - highest_score[..., None]), 0.0)
    total_weight = jnp.sum(weights, axis=-1)
    rounded = weights.astype(jnp.bfloat16)
    summed = jnp.einsum(
        "nkgm,mkd->nkgd", rounded, value_row_block, preferred_element_type=jnp.float32
    )
    layer_output = (summed / jnp.maximum(total_weight, 1.0)[..., None]).astype(jnp.bfloat16)
    return (highest_score, total_weight, layer_output)


def tile_partials(query_rows, query_req, query_pre, query_pos, bundle, tile_rows):
    key_row_block, value_row_block, key_pre, key_req, key_pos = bundle
    token_count = query_rows.shape[0]
    tile_count = token_count // tile_rows
    shaped = (
        query_rows.reshape((tile_count, tile_rows) + query_rows.shape[1:]),
        query_req.reshape(tile_count, tile_rows),
        query_pre.reshape(tile_count, tile_rows),
        query_pos.reshape(tile_count, tile_rows),
    )

    def one_tile(members):
        tile_queries, tile_req, tile_pre, tile_pos = members
        allowed = allowed_keys(tile_req, tile_pre, tile_pos, key_pre, key_req, key_pos)

        def computed(unused):
            return group_partial(tile_queries, allowed, key_row_block, value_row_block)

        def skipped(unused):
            stats_shape = tile_queries.shape[:-1]
            return (
                jnp.full(stats_shape, NEGATIVE_FLOOR, jnp.float32),
                jnp.zeros(stats_shape, jnp.float32),
                jnp.zeros(tile_queries.shape, jnp.bfloat16),
            )

        return lax.cond(jnp.any(allowed), computed, skipped, 0)

    highest_score, total_weight, layer_output = lax.map(one_tile, shaped)
    stats_shape = (token_count,) + query_rows.shape[1:-1]
    return (
        highest_score.reshape(stats_shape),
        total_weight.reshape(stats_shape),
        layer_output.reshape(query_rows.shape),
    )


def local(
    hidden_in,
    input_gain,
    w_query,
    key_value_weight,
    query_gain,
    key_gain,
    w_out,
    post_gain,
    w_gate,
    w_up,
    w_down,
    prefix_slot_cache,
    block_table,
    request_prefix,
    suffix_lengths,
):
    seq_count = lax.axis_size("seq")
    model_count = lax.axis_size("mp")
    my_seq = lax.axis_index("seq")
    my_model = lax.axis_index("mp")
    rows_here = hidden_in.shape[0]
    local_heads = w_query.shape[1] // HEAD_WIDTH
    group_width = QUERY_HEADS // KEY_VALUE_HEADS
    shared_heads = max(1, local_heads // group_width)
    query_per_head = local_heads // shared_heads
    pair_width = 2 * HEAD_WIDTH
    first_shared = my_model * local_heads // group_width
    blocks_here = prefix_slot_cache.shape[0]
    block_rows = prefix_slot_cache.shape[1]
    cache_extent = blocks_here * block_rows
    slot_total = blocks_here * seq_count
    prefix_length = slot_total // N_PREFIX * block_rows
    all_tokens = rows_here * seq_count
    hidden_f32 = hidden_in.astype(jnp.float32)
    normed = row_norm(hidden_f32, input_gain).astype(jnp.bfloat16)
    own_pos = my_seq * rows_here + jnp.arange(rows_here, dtype=jnp.int32)
    own_req, own_pre, own_rot = token_tables(request_prefix, suffix_lengths, own_pos, prefix_length)
    query_raw = jnp.dot(normed, w_query, preferred_element_type=jnp.float32).reshape(
        rows_here, local_heads, HEAD_WIDTH
    )
    query_rows_all = rotate(head_norm(query_raw, query_gain), own_rot).astype(jnp.bfloat16)
    pair_block = jnp.dot(normed, key_value_weight, preferred_element_type=jnp.float32).astype(
        jnp.bfloat16
    )
    share_ratio = max(1, group_width // local_heads)
    pair_split = pair_block.reshape(rows_here, shared_heads, 2, HEAD_WIDTH)
    key_row_block = rotate(
        head_norm(pair_split[:, :, 0].astype(jnp.float32), key_gain), own_rot
    ).astype(jnp.bfloat16)
    pairs_mine = jnp.stack([key_row_block, pair_split[:, :, 1]], axis=2).reshape(
        rows_here, shared_heads, pair_width
    )
    cache_cols = shared_heads * pair_width // share_ratio
    suffix_key_values = lax.dynamic_slice_in_dim(
        pairs_mine.reshape(rows_here, shared_heads * pair_width),
        my_model % share_ratio * cache_cols,
        cache_cols,
        1,
    )
    slot_ids = jnp.arange(slot_total, dtype=jnp.int32)
    owner_hits = (block_table[:, None] == slot_ids[None, :]).astype(jnp.int32)
    slot_prefix = jnp.sum(owner_hits * (slot_ids // (slot_total // N_PREFIX))[:, None], axis=0)
    cache_mine = lax.dynamic_slice_in_dim(prefix_slot_cache, first_shared, shared_heads, 2).reshape(
        cache_extent, shared_heads, pair_width
    )
    query_all = lax.all_gather(
        query_rows_all.reshape(rows_here, local_heads * HEAD_WIDTH), "seq", axis=0, tiled=True
    )
    query_all = query_all.reshape(all_tokens, shared_heads, query_per_head, HEAD_WIDTH)
    all_pos = jnp.arange(all_tokens, dtype=jnp.int32)
    all_req, all_pre, _ = token_tables(request_prefix, suffix_lengths, all_pos, prefix_length)
    group_pre = jnp.repeat(
        lax.dynamic_slice_in_dim(slot_prefix, my_seq * blocks_here, blocks_here), block_rows
    )
    key_positions = my_seq * rows_here + jnp.arange(rows_here, dtype=jnp.int32)
    group_req, _, _ = token_tables(request_prefix, suffix_lengths, key_positions, prefix_length)
    all_keys = jnp.concatenate([cache_mine[..., :HEAD_WIDTH], pairs_mine[..., :HEAD_WIDTH]], axis=0)
    all_values = jnp.concatenate(
        [cache_mine[..., HEAD_WIDTH:], pairs_mine[..., HEAD_WIDTH:]], axis=0
    )
    key_pre = jnp.concatenate([group_pre, jnp.full((rows_here,), -1, jnp.int32)])
    key_req = jnp.concatenate([jnp.full((cache_extent,), -1, jnp.int32), group_req])
    key_pos = jnp.concatenate([jnp.zeros((cache_extent,), jnp.int32), key_positions])
    bundle = (all_keys, all_values, key_pre, key_req, key_pos)
    highest_score, total_weight, layer_output = tile_partials(
        query_all, all_req, all_pre, all_pos, bundle, min(512, all_tokens)
    )
    highest_score = highest_score.reshape(seq_count, rows_here, shared_heads, query_per_head)
    total_weight = total_weight.reshape(seq_count, rows_here, shared_heads, query_per_head)
    layer_output = layer_output.reshape(
        seq_count, rows_here, shared_heads, query_per_head, HEAD_WIDTH
    )
    widened = lax.optimization_barrier(layer_output).astype(jnp.float32)
    result_back, peak_back, total_back = (
        lax.all_to_all(widened, "seq", split_axis=0, concat_axis=0, tiled=True),
        lax.all_to_all(highest_score, "seq", split_axis=0, concat_axis=0, tiled=True),
        lax.all_to_all(total_weight, "seq", split_axis=0, concat_axis=0, tiled=True),
    )
    best_score = jnp.max(peak_back, axis=0)
    scaling = total_back * jnp.exp(peak_back - best_score[None])
    attended = (
        jnp.sum(scaling[..., None] * result_back, axis=0) / jnp.sum(scaling, axis=0)[..., None]
    )
    attended = attended.astype(jnp.bfloat16).reshape(rows_here, local_heads * HEAD_WIDTH)
    partial_out = jnp.dot(attended, w_out, preferred_element_type=jnp.float32)
    column_count = hidden_in.shape[1] // model_count
    summed = lax.psum(partial_out.astype(jnp.bfloat16), "mp").astype(jnp.float32)
    residual = (hidden_f32 + summed).astype(jnp.bfloat16)
    residual_cols = lax.dynamic_slice_in_dim(residual, my_model * column_count, column_count, 1)
    post_normed = row_norm(residual.astype(jnp.float32), post_gain).astype(jnp.bfloat16)
    gate_terms = jnp.dot(post_normed, w_gate, preferred_element_type=jnp.float32)
    up_terms = jnp.dot(post_normed, w_up, preferred_element_type=jnp.float32)
    middle = (jax.nn.silu(gate_terms) * up_terms).astype(jnp.bfloat16)
    down_terms = jnp.dot(middle, w_down, preferred_element_type=jnp.float32)
    hidden_part = lax.psum_scatter(
        down_terms.astype(jnp.bfloat16), "mp", scatter_dimension=1, tiled=True
    ).astype(jnp.float32)
    hidden_out = (residual_cols.astype(jnp.float32) + hidden_part).astype(jnp.bfloat16)
    return (hidden_out, suffix_key_values)


def solution(mesh):
    in_specs = (
        P("seq", None),
        P(),
        P(None, "mp"),
        P(None, "mp"),
        P(),
        P(),
        P("mp", None),
        P(),
        P(None, "mp"),
        P(None, "mp"),
        P("mp", None),
        P("seq", None, None, None),
        P(),
        P(),
        P(),
    )
    out_specs = (P("seq", "mp"), P("seq", "mp"))
    return jax.shard_map(local, mesh=mesh, in_specs=in_specs, out_specs=out_specs, check_vma=False)
```

profile of v0, /device:TPU:2, one launch (start us, length us, event | category | flops | bytes accessed | tf_op | source)
XLA Modules:
  0.0 396.4 jit_solution(13331135312913714287)
XLA Ops:
  7.3 1.4 fusion.20
  8.7 1.8 convolution_convert_fusion.2
  12.8 36.2 %all_gather.3 = bf16[2048,128]{0,1:T(8,128)(2,1)S(1)} all-gather(bf16[128,128]{0,1:T(8,128)(2,1)S(1)} %pad_maximum_fusion.3), channel_id=1, replica_groups=mesh['seq'=16,'mp'=16] {'seq'}, dimensions={0}, use_global_device_ids=true | all-gather | bytes 557056 | tf_op jit(solution)/shard_map/all_gather | solution.py:191
  50.0 33.2 %while.14 = (s32[]{:T(128)}, f32[4,512,1,1]{1,3,2,0:T(1,128)S(1)}, f32[4,512,1,1]{1,3,2,0:T(1,128)}, bf16[4,512,1,1,128]{4,1,3,2,0:T(8,128)(2,1)}, s32[640]{0:T(...) while((s32[]{:T(128)}, f32[4,512,1,1]{1,3,2,0:T(1,128)S(1)}, ...), condition=%wide.region_15.16_spmd, body=%wide.region_9.15_spmd.sunk | while | flops 172817920 | bytes 6144739 | solution.py:116
  51.7 4.6 %conditional.2 = (f32[1,512,1,1]{1,3,2,0:T(1,128)}, f32[1,512,1,1]{1,3,2,0:T(1,128)}, bf16[1,512,1,1,128]{4,1,3,2,0:T(8,128)(2,1)S(1)}) conditional(s32[]{:T(128)} %convert_element_type.195, () %tuple.64, (pred[512,640]{1,0:T(32,128)(4,1)S(1)}, bf16[4,512,1,1,128]{4,1,3,2,0:T(8,128)(2,1)S(1)}, s32[]{:T(128)}, bf16[640,1,128]{2,0,1:T(8,128)(2,1)S(1)}, ...), branch_computations={%region_11.11_spmd, %region_12.14_spmd} | conditional | flops 170851840 | bytes 5519388 | solution.py:114
  52.8 1.7 fusion.5
  55.2 1.1 fusion.3
  56.3 1.3 constant_dynamic-update-slice_fusion.5
  60.0 4.6 %conditional.2 = (f32[1,512,1,1]{1,3,2,0:T(1,128)}, f32[1,512,1,1]{1,3,2,0:T(1,128)}, bf16[1,512,1,1,128]{4,1,3,2,0:T(8,128)(2,1)S(1)}) conditional(s32[]{:T(128)} %convert_element_type.195, () %tuple.64, (pred[512,640]{1,0:T(32,128)(4,1)S(1)}, bf16[4,512,1,1,128]{4,1,3,2,0:T(8,128)(2,1)S(1)}, s32[]{:T(128)}, bf16[640,1,128]{2,0,1:T(8,128)(2,1)S(1)}, ...), branch_computations={%region_11.11_spmd, %region_12.14_spmd} | conditional | flops 170851840 | bytes 5519388 | solution.py:114
  61.1 1.7 fusion.5
  63.5 1.1 fusion.3
  64.6 1.3 constant_dynamic-update-slice_fusion.5
  68.3 4.6 %conditional.2 = (f32[1,512,1,1]{1,3,2,0:T(1,128)}, f32[1,512,1,1]{1,3,2,0:T(1,128)}, bf16[1,512,1,1,128]{4,1,3,2,0:T(8,128)(2,1)S(1)}) conditional(s32[]{:T(128)} %convert_element_type.195, () %tuple.64, (pred[512,640]{1,0:T(32,128)(4,1)S(1)}, bf16[4,512,1,1,128]{4,1,3,2,0:T(8,128)(2,1)S(1)}, s32[]{:T(128)}, bf16[640,1,128]{2,0,1:T(8,128)(2,1)S(1)}, ...), branch_computations={%region_11.11_spmd, %region_12.14_spmd} | conditional | flops 170851840 | bytes 5519388 | solution.py:114
  68.3 1.1 fusion.66
  69.4 1.7 fusion.5
  71.8 1.1 fusion.3
  72.9 1.3 constant_dynamic-update-slice_fusion.5
  76.6 4.6 %conditional.2 = (f32[1,512,1,1]{1,3,2,0:T(1,128)}, f32[1,512,1,1]{1,3,2,0:T(1,128)}, bf16[1,512,1,1,128]{4,1,3,2,0:T(8,128)(2,1)S(1)}) conditional(s32[]{:T(128)} %convert_element_type.195, () %tuple.64, (pred[512,640]{1,0:T(32,128)(4,1)S(1)}, bf16[4,512,1,1,128]{4,1,3,2,0:T(8,128)(2,1)S(1)}, s32[]{:T(128)}, bf16[640,1,128]{2,0,1:T(8,128)(2,1)S(1)}, ...), branch_computations={%region_11.11_spmd, %region_12.14_spmd} | conditional | flops 170851840 | bytes 5519388 | solution.py:114
  77.6 1.7 fusion.5
  80.1 1.1 fusion.3
  81.2 1.3 constant_dynamic-update-slice_fusion.5
  83.1 12.5 %all_to_all.15 = f32[16,128,1,1]{1,3,2,0:T(1,128)S(1)} all-to-all(f32[16,128,1,1]{1,3,2,0:T(1,128)S(1)} %bitcast.115), channel_id=1, replica_groups=mesh['seq'=16,'mp'=16] {'seq'}, dimensions={0} | all-to-all | bytes 16384 | tf_op jit(solution)/shard_map/all_to_all | solution.py:221
  95.6 3.5 all-to-all-start
  99.1 2.1 convert_element_type.121
  101.2 7.7 %all-to-all-done = f32[16,128,1,1]{1,3,2,0:T(1,128)S(1)} async-done(((f32[16,128,1,1]{1,3,2,0:T(1,128)}), f32[16,128,1,1]{1,3,2,0:T(1,128)S(1)}, u32[]{:S(2)}, u32[]{:S(2)}) %all-to-all-start) | async-done | bytes 8224 | tf_op jit(solution)/shard_map/all_to_all | solution.py:222
  108.9 3.7 all-to-all-start.2
  112.7 20.4 %all-to-all-done.2 = f32[16,128,1,1,128]{4,1,3,2,0:T(8,128)S(1)} async-done(((f32[16,128,1,1,128]{4,1,3,2,0:T(8,128)}), f32[16,128,1,1,128]{4,1,3,2,0:T(8,128)S(1)}, u32[]{:S(2)}, u32[]{:S(2)}) %all-to-all-start.2) | async-done | bytes 1048608 | tf_op jit(solution)/shard_map/all_to_all | solution.py:220
  134.1 1.2 convolution_convert_fusion.1
  135.3 168.5 %all-reduce.5.cloned.1.call-done = bf16[128,2048]{1,0:T(8,128)(2,1)} async-done(((bf16[128,2048]{1,0:T(8,128)(2,1)}), bf16[128,2048]{1,0:T(8,128)(2,1)}) %all-reduce.5.cloned.1.call-update) | async-done | bytes 524304 | tf_op jit(solution)/shard_map/psum | solution.py:232
  303.9 1.4 fusion.17
  305.9 2.8 convolution_convert_fusion
  310.5 77.6 %reduce-scatter.4.cloned.1.call-done = bf16[128,128]{1,0:T(8,128)(2,1)} async-done(((bf16[2048,128]{1,0:T(8,128)(2,1)}), bf16[128,128]{1,0:T(8,128)(2,1)}) %reduce-scatter.4.cloned.1.call-update) | async-done | bytes 32784
  (110 shorter events, 21.0 us)
Async XLA Ops:
  7.2 42.1 %copy-start = (bf16[2,256,8,256]{3,2,1,0:T(8,128)(2,1)S(1)}, bf16[2,256,8,256]{3,2,1,0:T(8,128)(2,1)}, u32[]{:S(2)}) copy-start(bf16[2,256,8,256]{3,2,1,0:T(8,128)(2,1)} %param.30) | copy-start | bytes 6291460
  7.2 3.5 copy-start.12
  7.3 3.7 copy-start.6
  7.3 4.1 %copy-start.7 = (s32[32]{0:T(128)S(1)}, s32[32]{0:T(128)}, u32[]{:S(2)}) copy-start(s32[32]{0:T(128)} %param.32) | copy-start | bytes 388
  7.3 4.4 %copy-start.1 = (bf16[128,2048]{1,0:T(8,128)(2,1)S(1)}, bf16[128,2048]{1,0:T(8,128)(2,1)}, u32[]{:S(2)}) copy-start(bf16[128,2048]{1,0:T(8,128)(2,1)} %param.19) | copy-start | bytes 1572868
  7.3 4.4 %copy-start.9 = (bf16[2048,128]{1,0:T(8,128)(2,1)S(1)}, bf16[2048,128]{1,0:T(8,128)(2,1)}, u32[]{:S(2)}) copy-start(bf16[2048,128]{1,0:T(8,128)(2,1)} %param.21) | copy-start | bytes 1572868
  7.3 4.4 %copy-start.10 = (f32[2048]{0:T(1024)S(1)}, f32[2048]{0:T(1024)}, u32[]{:S(2)}) copy-start(f32[2048]{0:T(1024)} %param.20) | copy-start | bytes 24580
  10.5 1.6 copy-start.4
  10.5 1.7 copy-start.5
  95.6 13.3 %all-to-all-start = ((f32[16,128,1,1]{1,3,2,0:T(1,128)}), f32[16,128,1,1]{1,3,2,0:T(1,128)S(1)}, u32[]{:S(2)}, u32[]{:S(2)}) async-start(f32[16,128,1,1]{1,3,2,0:T(1,128)} %bitcast.29), calls=%async_computation | async-start | bytes 16384 | tf_op jit(solution)/shard_map/all_to_all | solution.py:222
  108.9 24.2 %all-to-all-start.2 = ((f32[16,128,1,1,128]{4,1,3,2,0:T(8,128)}), f32[16,128,1,1,128]{4,1,3,2,0:T(8,128)S(1)}, u32[]{:S(2)}, u32[]{:S(2)}) async-start(f32[16,128,1,1,128]{4,1,3,2,0:T(8,128)} %convert_element_type.121), calls=%async_computation.2 | async-start | bytes 2097152 | tf_op jit(solution)/shard_map/all_to_all | solution.py:220
  112.6 191.3 %all-reduce.5.cloned.1.call-start = ((), (), s32[]{:S(2)}) async-start(), calls=%async_computation.4 | async-start | bytes 1048576 | tf_op jit(solution)/shard_map/psum | solution.py:232
  133.1 1.0 copy-start.3
  133.4 170.4 %copy-start.2 = (bf16[128,2048]{1,0:T(8,128)(2,1)S(1)}, bf16[128,2048]{1,0:T(8,128)(2,1)}, u32[]{:S(2)}) copy-start(bf16[128,2048]{1,0:T(8,128)(2,1)} %param.19) | copy-start | bytes 1572868
  135.3 170.0 %copy-start.11 = (f32[2048]{0:T(1024)S(1)}, f32[2048]{0:T(1024)}, u32[]{:S(2)}) copy-start(f32[2048]{0:T(1024)} %param.26) | copy-start | bytes 24580
  135.3 252.8 %reduce-scatter.4.cloned.1.call-start = ((), (), s32[]{:S(2)}) async-start(), calls=%async_computation.5 | async-start | bytes 557056
  303.9 1.6 copy-start.8
Sparse Core Ops, SparseCore 0:
  135.4 168.3 all-reduce.4
  309.8 78.2 reduce-scatter.3
where the time goes:
time: 402 us; the launch traced here: 396 us
  waiting for transfers between devices  274 us (68%)
  blocking collectives  48.7 us (12%)
  other arithmetic  20.9 us (5%)
  matrix products  15.3 us (4%)
  between operations  14.5 us (4%)
  local copies, waits for them, and re-layouts  12.8 us (3%)
  starting transfers between devices  7.21 us (2%)
    psum x1, waiting for transfers between devices, local(): lax.psum(partial_out.astype(jnp.bfloat16), 'mp').astype(jnp.float32)  168 us
    unnamed x3, waiting for transfers between devices  77.6 us
    all_gather x1, blocking collectives, local(): lax.all_gather(query_rows_all.reshape(rows_here, local_heads * HEAD_WIDTH...  36.2 us
    all_to_all x1, waiting for transfers between devices, local(): lax.all_to_all(widened, 'seq', split_axis=0, concat_axis=0, tiled=True)  20.4 us
    all_to_all x1, blocking collectives, local(): lax.all_to_all(highest_score, 'seq', split_axis=0, concat_axis=0, tiled=T...  12.5 us
  transfers between devices with their start and end apart: 4, of which 4 were waited for; matrix products, arithmetic and copies ran while one was open for 1% of the time, Pallas kernels for 0%

commit v1 on v0

v1 whole, which is shorter than its diff:
```python
import math

import jax
import jax.numpy as jnp
from jax import lax
from jax.experimental import pallas as pl
from jax.experimental.pallas import tpu as pltpu
from jax.sharding import PartitionSpec as P

MESH = pl.DeviceIdType.MESH
HEAD = 128
TOK = 128
SEQ = 16
EPSILON = 1e-06
THETA = 1000000.0
FLOOR = -1e30
SCALE = math.log2(math.e) / math.sqrt(HEAD)
F32 = jnp.float32
BF16 = jnp.bfloat16


def dot(a, b, ca, cb):
    return lax.dot_general(a, b, (((ca,), (cb,)), ((), ())), preferred_element_type=F32)


def remote(src, dst, ss, rs, dev):
    return pltpu.make_async_remote_copy(
        src_ref=src, dst_ref=dst, send_sem=ss, recv_sem=rs, device_id=dev, device_id_type=MESH
    )


def row_scale(values):
    return lax.rsqrt(jnp.mean(values * values, axis=-1, keepdims=True) + EPSILON)


def slot_part(keys, values_t, queries, visible):
    scores = [dot(k, queries, 1, 1) for k in keys]
    peaks = [
        jnp.where(v, jnp.max(s, axis=0, keepdims=True) * SCALE, FLOOR)
        for s, v in zip(scores, visible)
    ]
    peak = jnp.maximum(peaks[0], peaks[1])
    total, out = None, None
    for s, v, vt in zip(scores, visible, values_t):
        weight = jnp.exp2(s * SCALE - jnp.where(v, peak, 1e30))
        part = jnp.sum(weight, axis=0, keepdims=True)
        prod = dot(vt, weight.astype(BF16), 1, 0)
        total = part if total is None else total + part
        out = prod if out is None else out + prod
    return peak, total, out


def kernel(
    table_ref,
    request_prefix_ref,
    lengths_ref,
    hidden_hbm,
    gain_hbm,
    post_gain_hbm,
    q_gain_ref,
    k_gain_ref,
    cos_ref,
    sin_ref,
    cache_ref,
    wq_hbm,
    wkv_hbm,
    wo_hbm,
    wg_hbm,
    wu_hbm,
    wd_hbm,
    out_ref,
    suffix_ref,
    hidden,
    gain,
    post_gain,
    wq,
    wkv,
    wo,
    wg,
    wu,
    wd,
    normed,
    peer_cache,
    vt,
    q_all,
    suf,
    half_out,
    half_stat,
    res_out,
    res_stat,
    back_out,
    back_stat,
    prefix_rows,
    part,
    part_x,
    part_z,
    sent_z,
    part2,
    part2_x,
    part2_z,
    sent2_z,
    gathered,
    dma_sem,
    kv_s,
    kv_r,
    suf_s,
    suf_r,
    q_s,
    q_r,
    o_s,
    o_r,
    st_s,
    st_r,
    x_s,
    x_r,
    z_s,
    z_r,
    x2_s,
    x2_r,
    z2_s,
    z2_r,
    g_s,
    g_r,
):
    s = lax.axis_index("seq")
    m = lax.axis_index("mp")
    y, zh, c = lax.div(s, 4), lax.rem(lax.div(s, 2), 2), lax.rem(s, 2)
    zl, x = lax.div(m, 4), lax.rem(m, 4)

    def at_seq(i):
        return {"seq": i}

    def at_mp(i):
        return {"mp": i}

    loads = []
    for k, (src, dst) in enumerate(
        [
            (hidden_hbm, hidden),
            (gain_hbm, gain),
            (wq_hbm, wq),
            (wkv_hbm, wkv),
            (wo_hbm, wo),
            (post_gain_hbm, post_gain),
            (wg_hbm, wg),
            (wu_hbm, wu),
            (wd_hbm, wd),
        ]
    ):
        copy = pltpu.make_async_copy(src, dst, dma_sem.at[k])
        copy.start()
        loads.append(copy)

    z_peer = at_seq(y * 4 + (1 - zh) * 2 + c)
    yc_peers = []
    for dy, dc in ((0, 1), (1, 0), (1, 1), (3, 0), (3, 1), (2, 0), (2, 1)):
        yy, cc = lax.rem(y + dy, 4), lax.rem(c + dc, 2)
        yc_peers.append((yy * 2 + cc, at_seq(yy * 4 + zh * 2 + cc)))
    mine = y * 2 + c
    after = [at_seq(lax.rem(s + 2, SEQ)), at_seq(lax.rem(s + 1, SEQ))]
    before = [at_seq(lax.rem(s + 14, SEQ)), at_seq(lax.rem(s + 15, SEQ))]
    hops = (2, 1, 3)
    x_peers = [at_mp(zl * 4 + lax.rem(x + i, 4)) for i in hops]
    z_peers = [at_mp(lax.rem(zl + i, 4) * 4 + x) for i in hops]

    barrier = pltpu.get_barrier_semaphore()
    everyone = [z_peer] + [p for _, p in yc_peers] + after + before + x_peers + z_peers
    for dev in everyone:
        pl.semaphore_signal(barrier, inc=1, device_id=dev, device_id_type=MESH)

    token = lax.broadcasted_iota(jnp.int32, (SEQ, TOK), 0) * TOK + lax.broadcasted_iota(
        jnp.int32, (SEQ, TOK), 1
    )
    own_token = s * TOK + lax.broadcasted_iota(jnp.int32, (1, TOK), 1)
    prefix = jnp.zeros((SEQ, TOK), jnp.int32)
    own_start = jnp.zeros((1, TOK), jnp.int32)
    begin = jnp.int32(0)
    for r in range(32):
        end = begin + lengths_ref[r]
        prefix = jnp.where((token >= begin) & (token < end), request_prefix_ref[r], prefix)
        own_start = jnp.where((own_token >= begin) & (own_token < end), begin, own_start)
        begin = end
    prefix_rows[...] = prefix

    slot_ids = [2 * s, 2 * s + 1, 2 * s + 4 - 8 * zh, 2 * s + 5 - 8 * zh]
    slot_prefix = [jnp.int32(0)] * 4
    for i in range(32):
        held = table_ref[i]
        slot_prefix = [
            jnp.where(held == slot, jnp.int32(i // 8), p) for slot, p in zip(slot_ids, slot_prefix)
        ]

    loads[0].wait()
    loads[1].wait()
    raw = hidden[...].astype(F32)
    normed[...] = (raw * row_scale(raw) * gain[...]).astype(BF16)

    pl.semaphore_wait(barrier, len(everyone))

    kv_copies = []
    for b in range(2):
        rows = pl.ds(b * 256, 256)
        copy = remote(cache_ref.at[rows], peer_cache.at[rows], kv_s.at[b], kv_r.at[b], z_peer)
        copy.start()
        kv_copies.append(copy)

    cosine, sine = cos_ref[...], sin_ref[...]

    def head_rope(values, g):
        scaled = values * row_scale(values) * g
        return (scaled * cosine + pltpu.roll(scaled, HEAD // 2, 1) * sine).astype(BF16)

    loads[2].wait()
    q_raw = dot(normed[...], wq[...], 1, 0)
    q_all[mine] = head_rope(q_raw, q_gain_ref[...])
    q_copies = []
    for k, (_, dev) in enumerate(yc_peers):
        copy = remote(q_all.at[mine], q_all.at[mine], q_s.at[k], q_r.at[mine], dev)
        copy.start()
        q_copies.append(copy)

    loads[3].wait()
    pair = dot(normed[...], wkv[...], 1, 0).astype(BF16)
    key_rows = head_rope(pair[:, :HEAD].astype(F32), k_gain_ref[...])
    value_rows = pair[:, HEAD:]
    suf[2, 0] = key_rows
    suf[2, 1] = value_rows.T
    suf_copies = []
    for k in range(2):
        copy = remote(suf.at[2], suf.at[k], suf_s.at[k], suf_r.at[k], after[k])
        copy.start()
        suf_copies.append(copy)
    suffix_ref[...] = jnp.where(lax.rem(m, 2) == 0, key_rows, value_rows)

    for b in range(2):
        vt[b] = cache_ref[pl.ds(b * 256, 256), pl.ds(HEAD, HEAD)].T

    def block_of(j):
        yy = lax.rem(y + lax.div(j, 2), 4)
        cc = lax.rem(c + lax.rem(j, 2), 2)
        return yy * 2 + cc, yy * 4 + zh * 2 + cc

    def attend(block, tokens, cache, first):
        queries = q_all[block]
        pre = prefix_rows[pl.ds(tokens, 1), :]
        return slot_part(
            [cache[pl.ds(b * 256, 256), pl.ds(0, HEAD)] for b in range(2)],
            [vt[first + b] for b in range(2)],
            queries,
            [pre == slot_prefix[first + b] for b in range(2)],
        )

    def first_half(j, carry):
        block, tokens = block_of(j)

        @pl.when(j > 0)
        def _():
            remote(q_all.at[block], q_all.at[block], q_s.at[0], q_r.at[block], z_peer).wait_recv()

        peak, total, out = attend(block, tokens, cache_ref, 0)
        half_stat[j, pl.ds(0, 1), :] = peak
        half_stat[j, pl.ds(1, 1), :] = total
        half_out[j] = out
        return carry

    lax.fori_loop(0, 8, first_half, 0)

    for copy in suf_copies:
        copy.wait_recv()
    queries = q_all[mine]
    suffix_scores = []
    for k in range(3):
        at = (s - 2 + k) * TOK + lax.broadcasted_iota(jnp.int32, (TOK, TOK), 0)
        seen = (at >= own_start) & (at <= own_token)
        suffix_scores.append(
            jnp.where(seen, dot(suf[k, 0], queries, 1, 1) * SCALE, FLOOR)
        )
    suffix_peak = jnp.max(
        jnp.maximum(jnp.maximum(suffix_scores[0], suffix_scores[1]), suffix_scores[2]),
        axis=0,
        keepdims=True,
    )
    suffix_total = jnp.zeros((1, TOK), F32)
    suffix_out = jnp.zeros((HEAD, TOK), F32)
    for k in range(3):
        weight = jnp.exp2(suffix_scores[k] - suffix_peak)
        suffix_total += jnp.sum(weight, axis=0, keepdims=True)
        suffix_out += dot(suf[k, 1], weight.astype(BF16), 1, 0)

    for copy in kv_copies:
        copy.wait_recv()
    for b in range(2):
        vt[2 + b] = peer_cache[pl.ds(b * 256, 256), pl.ds(HEAD, HEAD)].T

    def second_half(i, carry):
        j = 7 - i
        block, tokens = block_of(j)
        peak1, total1, out1 = attend(block, tokens, peer_cache, 2)
        peak0 = half_stat[j, pl.ds(0, 1), :]
        total0 = half_stat[j, pl.ds(1, 1), :]
        peak = jnp.maximum(peak0, peak1)
        f0, f1 = jnp.exp2(peak0 - peak), jnp.exp2(peak1 - peak)
        total = total0 * f0 + total1 * f1
        inverse = 1.0 / jnp.maximum(total, 1.0)
        res_out[block] = (half_out[j] * (f0 * inverse) + out1 * (f1 * inverse)).astype(BF16)
        res_stat[block, pl.ds(0, 1), :] = peak
        res_stat[block, pl.ds(1, 1), :] = total

        @pl.when(j > 0)
        def _():
            dev = at_seq(tokens)
            remote(
                res_out.at[block], back_out.at[mine], o_s.at[block], o_r.at[mine], dev
            ).start()
            remote(
                res_stat.at[block], back_stat.at[mine], st_s.at[block], st_r.at[mine], dev
            ).start()

        return carry

    lax.fori_loop(0, 8, second_half, 0)

    parts = [(suffix_peak, suffix_total, suffix_out / suffix_total)]
    parts.append((res_stat[mine, pl.ds(0, 1), :], res_stat[mine, pl.ds(1, 1), :], res_out[mine]))
    for block, dev in yc_peers:
        remote(res_out.at[block], back_out.at[block], o_s.at[block], o_r.at[block], dev).wait_recv()
        remote(
            res_stat.at[block], back_stat.at[block], st_s.at[block], st_r.at[block], dev
        ).wait_recv()
        parts.append(
            (back_stat[block, pl.ds(0, 1), :], back_stat[block, pl.ds(1, 1), :], back_out[block])
        )
    best = parts[0][0]
    for peak, _, _ in parts[1:]:
        best = jnp.maximum(best, peak)
    weight_sum, accumulated = None, None
    for peak, total, out in parts:
        factor = total * jnp.exp2(peak - best)
        term = factor * out.astype(F32)
        weight_sum = factor if weight_sum is None else weight_sum + factor
        accumulated = term if accumulated is None else accumulated + term
    attended = (accumulated / weight_sum).astype(BF16)
    attended = attended.T

    def reduce_scatter(left, weight, blocks, from_x, from_z, to_z, xs, xr, zs, zr):
        sends = []
        for i in (2, 1, 3, 0):
            zz = lax.rem(zl + i, 4)
            prod = dot(left, weight[:, pl.ds(pl.multiple_of(zz * 512, 512), 512)], 1, 0)
            prod = prod.astype(BF16)
            for k in range(4):
                blocks[i, k] = prod[:, k * HEAD : (k + 1) * HEAD]
            for k, hop in enumerate(hops):
                copy = remote(
                    blocks.at[i, lax.rem(x + hop, 4)],
                    from_x.at[i, k],
                    xs.at[i, k],
                    xr.at[i, k],
                    x_peers[k],
                )
                copy.start()
                sends.append(copy)
        z_sends = []
        for n, i in enumerate((2, 1, 3, 0)):
            for k in range(3):
                sends[n * 3 + k].wait_recv()
            acc = blocks[i, x].astype(F32)
            for k in range(3):
                acc = acc + from_x[i, k].astype(F32)
            if i:
                to_z[n] = acc.astype(BF16)
                copy = remote(to_z.at[n], from_z.at[n], zs.at[n], zr.at[n], z_peers[n])
                copy.start()
                z_sends.append(copy)
        for n, copy in enumerate(z_sends):
            copy.wait_recv()
            acc = acc + from_z[n].astype(F32)
        return acc, sends + z_sends

    loads[4].wait()
    summed, sends1 = reduce_scatter(
        attended, wo, part, part_x, part_z, sent_z, x_s, x_r, z_s, z_r
    )
    columns = pl.ds(pl.multiple_of(m * HEAD, HEAD), HEAD)
    residual = (hidden[:, columns].astype(F32) + summed).astype(BF16)

    gathered[m] = residual
    g_copies = []

    def share(block, dev):
        n = len(g_copies)
        copy = remote(gathered.at[block], gathered.at[block], g_s.at[n], g_r.at[block], dev)
        copy.start()
        g_copies.append(copy)

    def arrived(block):
        remote(
            gathered.at[block], gathered.at[block], g_s.at[0], g_r.at[block], z_peers[0]
        ).wait_recv()

    for dev in z_peers:
        share(m, dev)
    for dev in x_peers:
        share(m, dev)
    for i in (1, 3, 2):
        block = lax.rem(zl + i, 4) * 4 + x
        arrived(block)
        for dev in x_peers:
            share(block, dev)
    for i in (1, 3, 2):
        for zz in range(4):
            arrived(zz * 4 + lax.rem(x + i, 4))

    square = jnp.zeros((TOK, HEAD), F32)
    for k in range(16):
        v = gathered[k].astype(F32)
        square = square + v * v
    scale = lax.rsqrt(jnp.sum(square, axis=-1, keepdims=True) * (1.0 / 2048) + EPSILON)
    loads[5].wait()
    for k in range(16):
        cols = pl.ds(k * HEAD, HEAD)
        normed[:, cols] = (gathered[k].astype(F32) * scale * post_gain[:, cols]).astype(BF16)
    loads[6].wait()
    gate = dot(normed[...], wg[...], 1, 0)
    loads[7].wait()
    up = dot(normed[...], wu[...], 1, 0)
    middle = (gate / (1.0 + jnp.exp(-gate)) * up).astype(BF16)
    loads[8].wait()
    summed, sends2 = reduce_scatter(
        middle, wd, part2, part2_x, part2_z, sent2_z, x2_s, x2_r, z2_s, z2_r
    )
    out_ref[...] = (residual.astype(F32) + summed).astype(BF16)

    for copy in kv_copies + suf_copies + q_copies + sends1 + sends2 + g_copies:
        copy.wait_send()
    for block, dev in yc_peers:
        remote(res_out.at[block], back_out.at[block], o_s.at[block], o_r.at[block], dev).wait_send()
        remote(
            res_stat.at[block], back_stat.at[block], st_s.at[block], st_r.at[block], dev
        ).wait_send()


def local(
    hidden_in,
    input_gain,
    w_query,
    key_value_weight,
    query_gain,
    key_gain,
    w_out,
    post_gain,
    w_gate,
    w_up,
    w_down,
    prefix_slot_cache,
    block_table,
    request_prefix,
    suffix_lengths,
):
    my_seq = lax.axis_index("seq")
    my_model = lax.axis_index("mp")
    own = my_seq * TOK + jnp.arange(TOK, dtype=jnp.int32)
    ends = jnp.cumsum(suffix_lengths)
    starts = ends - suffix_lengths
    inside = (own[:, None] >= starts[None, :]) & (own[:, None] < ends[None, :])
    start_of = jnp.sum(inside.astype(jnp.int32) * starts[None, :], axis=1)
    rotary_pos = (2048 + own - start_of).astype(F32)
    half = HEAD // 2
    inverse = jnp.exp(jnp.arange(half).astype(F32) * (-2.0 * math.log(THETA) / HEAD))
    angles = rotary_pos[:, None] * inverse[None, :]
    cosine, sine = jnp.cos(angles), jnp.sin(angles)
    cosine = jnp.concatenate([cosine, cosine], axis=1)
    sine = jnp.concatenate([-sine, sine], axis=1)
    cache = lax.dynamic_slice_in_dim(prefix_slot_cache, my_model // 2, 1, 2).reshape(512, 2 * HEAD)

    vmem = pl.BlockSpec(memory_space=pltpu.VMEM)
    smem = pl.BlockSpec(memory_space=pltpu.SMEM)
    hbm = pl.BlockSpec(memory_space=pl.ANY)
    V = pltpu.VMEM
    D = pltpu.SemaphoreType.DMA
    block = (TOK, HEAD)
    return pl.pallas_call(
        kernel,
        out_shape=(
            jax.ShapeDtypeStruct((TOK, HEAD), BF16),
            jax.ShapeDtypeStruct((TOK, HEAD), BF16),
        ),
        in_specs=[smem] * 3 + [hbm] * 3 + [vmem] * 5 + [hbm] * 6,
        out_specs=(vmem, vmem),
        scratch_shapes=[
            V((128, 2048), BF16),
            V((1, 2048), F32),
            V((1, 2048), F32),
            V((2048, 128), BF16),
            V((2048, 256), BF16),
            V((128, 2048), BF16),
            V((2048, 384), BF16),
            V((2048, 384), BF16),
            V((384, 2048), BF16),
            V((128, 2048), BF16),
            V((512, 256), BF16),
            V((4, 128, 256), BF16),
            V((8,) + block, BF16),
            V((3, 2) + block, BF16),
            V((8,) + block, F32),
            V((8, 8, 128), F32),
            V((8,) + block, BF16),
            V((8, 8, 128), F32),
            V((8,) + block, BF16),
            V((8, 8, 128), F32),
            V((16, 128), jnp.int32),
            V((4, 4) + block, BF16),
            V((4, 3) + block, BF16),
            V((3,) + block, BF16),
            V((3,) + block, BF16),
            V((4, 4) + block, BF16),
            V((4, 3) + block, BF16),
            V((3,) + block, BF16),
            V((3,) + block, BF16),
            V((16,) + block, BF16),
            D((9,)),
            D((2,)),
            D((2,)),
            D((2,)),
            D((2,)),
            D((7,)),
            D((8,)),
            D((8,)),
            D((8,)),
            D((8,)),
            D((8,)),
            D((4, 3)),
            D((4, 3)),
            D((3,)),
            D((3,)),
            D((4, 3)),
            D((4, 3)),
            D((3,)),
            D((3,)),
            D((15,)),
            D((16,)),
        ],
        compiler_params=pltpu.CompilerParams(
            collective_id=0, has_side_effects=True, vmem_limit_bytes=48 * 1024 * 1024
        ),
        name="layer",
    )(
        block_table,
        request_prefix,
        suffix_lengths,
        hidden_in,
        input_gain.reshape(1, -1),
        post_gain.reshape(1, -1),
        query_gain.reshape(1, -1),
        key_gain.reshape(1, -1),
        cosine,
        sine,
        cache,
        w_query,
        key_value_weight,
        w_out,
        w_gate,
        w_up,
        w_down,
    )


def solution(mesh):
    in_specs = (
        P("seq", None),
        P(),
        P(None, "mp"),
        P(None, "mp"),
        P(),
        P(),
        P("mp", None),
        P(),
        P(None, "mp"),
        P(None, "mp"),
        P("mp", None),
        P("seq", None, None, None),
        P(),
        P(),
        P(),
    )
    out_specs = (P("seq", "mp"), P("seq", "mp"))
    return jax.shard_map(local, mesh=mesh, in_specs=in_specs, out_specs=out_specs, check_vma=False)
```

time: 402 us -> 78.2 us (0.19); the launches traced: 396 us -> 77.6 us
  waiting for transfers between devices: 274 us -> 0 us
  Pallas kernels: 0 us -> 68.1 us
  blocking collectives: 48.7 us -> 0 us
  other arithmetic: 20.9 us -> 0.7 us
  matrix products: 15.3 us -> 0 us
  between operations: 14.5 us -> 0.86 us
  starting transfers between devices: 7.21 us -> 0 us
  local copies, waits for them, and re-layouts: 12.8 us -> 7.96 us
    psum x1 -> x0, waiting for transfers between devices: 168 us -> none  [local(): lax.psum(partial_out.astype(jnp.bfloat16), 'mp').astype(jnp.float32)]
    unnamed x3 -> x0, waiting for transfers between devices: 77.6 us -> none
    pallas_call x0 -> x1, Pallas kernels: none -> 68.1 us  [local(): pl.pallas_call(kernel, out_shape=(jax.ShapeDtypeStruct((TOK, HEAD), BF16)...]
    all_gather x1 -> x0, blocking collectives: 36.2 us -> none  [local(): lax.all_gather(query_rows_all.reshape(rows_here, local_heads * HEAD_WIDTH...]
    all_to_all x2 -> x0, waiting for transfers between devices: 28.1 us -> none  [the longest x1 20.4 us: local(): lax.all_to_all(widened, 'seq', split_axis=0, concat_axis=0, tiled=True)]
    dot_general x13 -> x0, matrix products: 15.3 us -> none  [the longest x4 4.48 us: group_partial(): jnp.einsum('nkgm,mkd->nkgd', rounded, value_row_block, preferred_element_...]
    all_to_all x1 -> x0, blocking collectives: 12.5 us -> none  [local(): lax.all_to_all(highest_score, 'seq', split_axis=0, concat_axis=0, tiled=T...]
    reduce_sum x12 -> x1, other arithmetic: 10.5 us -> 0.09 us  [local(): start_of = jnp.sum(inside.astype(jnp.int32) * starts[None, :], axis=1)]
  transfers between devices with their start and end apart: 4 -> 0, of which waited for: 4 -> 0; matrix products, arithmetic and copies ran while one was open for 1% -> 0% of each run, Pallas kernels for 0% -> 0%
where the time goes in v1:
time: 78.2 us; the launch traced here: 77.6 us
  Pallas kernels  68.1 us (87%)
  local copies, waits for them, and re-layouts  7.96 us (10%)
  between operations  0.86 us (1%)
    pallas_call x1, Pallas kernels, local(): pl.pallas_call(kernel, out_shape=(jax.ShapeDtypeStruct((TOK, HEAD), BF16)...  68.1 us
    unnamed x29, local copies, waits for them, and re-layouts  7.32 us

profile of v1, /device:TPU:2, one launch (start us, length us, event | category | flops | bytes accessed | tf_op | source)
XLA Modules:
  0.0 77.6 jit_solution(9878302475562281546)
XLA Ops:
  0.6 0.0 copy-start
  0.6 0.0 copy-start.8
  0.7 0.0 copy-start.6
  0.7 0.0 copy-start.7
  0.7 0.0 copy-start.11
  0.7 0.0 copy-start.12
  0.7 0.0 copy-start.2
  0.7 0.0 copy-start.9
  0.7 0.0 copy-start.10
  0.7 1.5 %copy-done = bf16[2,256,8,256]{3,2,1,0:T(8,128)(2,1)S(1)} copy-done((bf16[2,256,8,256]{3,2,1,0:T(8,128)(2,1)S(1)}, bf16[2,256,8,256]{3,2,1,0:T(8,128)(2,1)}, u32[]{:S(2)}) %copy-start) | copy-done | bytes 2097176
  2.2 0.5 constant_dynamic-slice_fusion
  2.8 0.0 copy-done.8
  2.9 0.1 copy.20
  2.9 0.1 reduce-window.8
  3.0 0.1 reduce
  3.1 0.1 select_reduce_fusion
  3.2 0.3 fusion
  3.6 0.1 pad_maximum_fusion
  3.7 0.0 copy-done.6
  3.7 0.0 copy-done.7
  3.7 0.0 copy-done.11
  3.7 0.0 copy-done.12
  3.7 0.0 copy-done.2
  3.7 0.0 copy-done.9
  3.7 0.0 copy-start.1
  3.7 1.4 %copy-done.1 = bf16[2048,384]{1,0:T(8,128)(2,1)S(1)} copy-done((bf16[2048,384]{1,0:T(8,128)(2,1)S(1)}, bf16[2048,384]{1,0:T(8,128)(2,1)}, u32[]{:S(2)}) %copy-start.1) | copy-done | bytes 1572888
  5.2 1.0 %copy-done.3 = bf16[128,2048]{1,0:T(8,128)(2,1)S(1)} copy-done((bf16[128,2048]{1,0:T(8,128)(2,1)S(1)}, bf16[128,2048]{1,0:T(8,128)(2,1)}, u32[]{:S(2)}) %copy-start.3) | copy-done | bytes 524312
  6.2 1.0 %copy-done.4 = bf16[2048,128]{1,0:T(8,128)(2,1)S(1)} copy-done((bf16[2048,128]{1,0:T(8,128)(2,1)S(1)}, bf16[2048,128]{1,0:T(8,128)(2,1)}, u32[]{:S(2)}) %copy-start.4) | copy-done | bytes 524312
  7.2 1.0 %copy-done.5 = bf16[128,2048]{1,0:T(8,128)(2,1)S(1)} copy-done((bf16[128,2048]{1,0:T(8,128)(2,1)S(1)}, bf16[128,2048]{1,0:T(8,128)(2,1)}, u32[]{:S(2)}) %copy-start.5) | copy-done | bytes 524312
  8.3 68.1 %layer.1 = (bf16[128,128]{1,0:T(8,128)(2,1)S(1)}, bf16[128,128]{1,0:T(8,128)(2,1)S(1)}) custom-call(s32[32]{0:T(128)S(1)} %copy-done.9, s32[32]{0:T(128)S(1)} %copy-done.10, s32[32]{0:T(128)S(1)} %copy-done.8, bf16[128,2048]{1,0:T(8,128)(2,1)S(1)} %copy-done.3, f32[1,2048]{1,0:T(1,128)S(1)} %bitcast.7, f32[1,2048]{1,0:T(1,128)S(1)} %bitcast.8, ...), custom_call_target="tpu_custom_call" | custom-call | tf_op jit(solution)/shard_map/layer/pallas_call | solution.py:482
  76.4 0.6 copy.25
  77.0 0.6 copy.26
  (9 shorter events, 0.1 us)
Async XLA Ops:
  0.6 1.6 %copy-start = (bf16[2,256,8,256]{3,2,1,0:T(8,128)(2,1)S(1)}, bf16[2,256,8,256]{3,2,1,0:T(8,128)(2,1)}, u32[]{:S(2)}) copy-start(bf16[2,256,8,256]{3,2,1,0:T(8,128)(2,1)} %param.26) | copy-start | bytes 6291460
  0.6 2.2 %copy-start.8 = (s32[32]{0:T(128)S(1)}, s32[32]{0:T(128)}, u32[]{:S(2)}) copy-start(s32[32]{0:T(128)} %lengths_ref.1) | copy-start | bytes 388
  0.7 3.0 %copy-start.6 = (f32[2048]{0:T(1024)S(1)}, f32[2048]{0:T(1024)}, u32[]{:S(2)}) copy-start(f32[2048]{0:T(1024)} %param.16) | copy-start | bytes 24580
  0.7 3.0 %copy-start.7 = (f32[2048]{0:T(1024)S(1)}, f32[2048]{0:T(1024)}, u32[]{:S(2)}) copy-start(f32[2048]{0:T(1024)} %param.22) | copy-start | bytes 24580
  0.7 3.0 %copy-start.11 = (f32[128]{0:T(128)S(1)}, f32[128]{0:T(128)}, u32[]{:S(2)}) copy-start(f32[128]{0:T(128)} %param.19) | copy-start | bytes 1540
  0.7 3.0 %copy-start.12 = (f32[128]{0:T(128)S(1)}, f32[128]{0:T(128)}, u32[]{:S(2)}) copy-start(f32[128]{0:T(128)} %param.20) | copy-start | bytes 1540
  0.7 3.0 %copy-start.2 = (bf16[2048,256]{1,0:T(8,128)(2,1)S(1)}, bf16[2048,256]{1,0:T(8,128)(2,1)}, u32[]{:S(2)}) copy-start(bf16[2048,256]{1,0:T(8,128)(2,1)} %wkv_hbm.1) | copy-start | bytes 3145732
  0.7 3.0 %copy-start.9 = (s32[32]{0:T(128)S(1)}, s32[32]{0:T(128)}, u32[]{:S(2)}) copy-start(s32[32]{0:T(128)} %table_ref.1) | copy-start | bytes 388
  0.7 3.0 %copy-start.10 = (s32[32]{0:T(128)S(1)}, s32[32]{0:T(128)}, u32[]{:S(2)}) copy-start(s32[32]{0:T(128)} %request_prefix_ref.1) | copy-start | bytes 388
  3.7 1.4 %copy-start.1 = (bf16[2048,384]{1,0:T(8,128)(2,1)S(1)}, bf16[2048,384]{1,0:T(8,128)(2,1)}, u32[]{:S(2)}) copy-start(bf16[2048,384]{1,0:T(8,128)(2,1)} %wg_hbm.1) | copy-start | bytes 4718596
  5.1 1.0 %copy-start.3 = (bf16[128,2048]{1,0:T(8,128)(2,1)S(1)}, bf16[128,2048]{1,0:T(8,128)(2,1)}, u32[]{:S(2)}) copy-start(bf16[128,2048]{1,0:T(8,128)(2,1)} %hidden_hbm.1) | copy-start | bytes 1572868
  6.2 1.0 %copy-start.4 = (bf16[2048,128]{1,0:T(8,128)(2,1)S(1)}, bf16[2048,128]{1,0:T(8,128)(2,1)}, u32[]{:S(2)}) copy-start(bf16[2048,128]{1,0:T(8,128)(2,1)} %wq_hbm.1) | copy-start | bytes 1572868
  7.2 1.0 %copy-start.5 = (bf16[128,2048]{1,0:T(8,128)(2,1)S(1)}, bf16[128,2048]{1,0:T(8,128)(2,1)}, u32[]{:S(2)}) copy-start(bf16[128,2048]{1,0:T(8,128)(2,1)} %wo_hbm.1) | copy-start | bytes 1572868

commit v2 on v1

--- a/solution.py
+++ b/solution.py
@@ -1,3 +1,4 @@
+import functools
 import math
 
 import jax
@@ -80,7 +81,7 @@
     wu,
     wd,
     normed,
-    peer_cache,
+    kk,
     vt,
     q_all,
     suf,
@@ -103,6 +104,8 @@
     dma_sem,
     kv_s,
     kv_r,
+    kx_s,
+    kx_r,
     suf_s,
     suf_r,
     q_s,
@@ -155,8 +158,10 @@
     yc_peers = []
     for dy, dc in ((0, 1), (1, 0), (1, 1), (3, 0), (3, 1), (2, 0), (2, 1)):
         yy, cc = lax.rem(y + dy, 4), lax.rem(c + dc, 2)
-        yc_peers.append((yy * 2 + cc, at_seq(yy * 4 + zh * 2 + cc)))
-    mine = y * 2 + c
+        yc_peers.append((cc * 4 + yy, at_seq(yy * 4 + zh * 2 + cc)))
+    mine = c * 4 + y
+    px = lax.rem(x, 2)
+    x_partner = at_mp(zl * 4 + x + 1 - 2 * px)
     after = [at_seq(lax.rem(s + 2, SEQ)), at_seq(lax.rem(s + 1, SEQ))]
     before = [at_seq(lax.rem(s + 14, SEQ)), at_seq(lax.rem(s + 15, SEQ))]
     hops = (2, 1, 3)
@@ -168,11 +173,12 @@
     for dev in everyone:
         pl.semaphore_signal(barrier, inc=1, device_id=dev, device_id_type=MESH)
 
-    token = lax.broadcasted_iota(jnp.int32, (SEQ, TOK), 0) * TOK + lax.broadcasted_iota(
-        jnp.int32, (SEQ, TOK), 1
-    )
+    lane = lax.broadcasted_iota(jnp.int32, (8, 512), 1)
+    core = lax.broadcasted_iota(jnp.int32, (8, 512), 0)
+    block_at = lax.shift_right_logical(lane, 7) * 4 + zh * 2 + core
+    token = block_at * TOK + (lane & 127)
     own_token = s * TOK + lax.broadcasted_iota(jnp.int32, (1, TOK), 1)
-    prefix = jnp.zeros((SEQ, TOK), jnp.int32)
+    prefix = jnp.zeros((8, 512), jnp.int32)
     own_start = jnp.zeros((1, TOK), jnp.int32)
     begin = jnp.int32(0)
     for r in range(32):
@@ -195,14 +201,18 @@
     raw = hidden[...].astype(F32)
     normed[...] = (raw * row_scale(raw) * gain[...]).astype(BF16)
 
+    for b in range(2):
+        kk[b] = cache_ref[pl.ds(b * 256, 256), pl.ds(0, HEAD)]
+        vt[b] = cache_ref[pl.ds(b * 256, 256), pl.ds(HEAD, HEAD)].T
+
     pl.semaphore_wait(barrier, len(everyone))
 
-    kv_copies = []
-    for b in range(2):
-        rows = pl.ds(b * 256, 256)
-        copy = remote(cache_ref.at[rows], peer_cache.at[rows], kv_s.at[b], kv_r.at[b], z_peer)
+    kv_copies = [
+        remote(ref.at[px], ref.at[2 + px], kv_s.at[b], kv_r.at[b], z_peer)
+        for b, ref in enumerate((kk, vt))
+    ]
+    for copy in kv_copies:
         copy.start()
-        kv_copies.append(copy)
 
     cosine, sine = cos_ref[...], sin_ref[...]
 
@@ -225,45 +235,67 @@
     value_rows = pair[:, HEAD:]
     suf[2, 0] = key_rows
     suf[2, 1] = value_rows.T
+    suffix_ref[...] = jnp.where(lax.rem(m, 2) == 0, key_rows, value_rows)
+
+    pass_copies = []
+    for b, ref in enumerate((kk, vt)):
+        kv_copies[b].wait_recv()
+        copy = remote(ref.at[2 + px], ref.at[2 + px], kx_s.at[b], kx_r.at[b], x_partner)
+        copy.start()
+        pass_copies.append(copy)
+
+    def attend(core, first):
+        return slot_part(
+            [kk[first + b] for b in range(2)],
+            [vt[first + b] for b in range(2)],
+            q_all[pl.ds(core * 4, 4)].reshape(512, HEAD),
+            [prefix_rows[pl.ds(core, 1), :] == slot_prefix[first + b] for b in range(2)],
+        )
+
+    def q_arrived(k, core):
+        block = core * 4 + lax.rem(y + k, 4)
+        remote(q_all.at[block], q_all.at[block], q_s.at[0], q_r.at[block], z_peer).wait_recv()
+
+    for core in range(2):
+        for k in (1, 3, 2):
+            q_arrived(k, core)
+        pl.when(c != core)(functools.partial(q_arrived, 0, core))
+        peak, total, out = attend(core, 0)
+        half_stat[core, pl.ds(0, 1), :] = peak
+        half_stat[core, pl.ds(1, 1), :] = total
+        half_out[core] = out
+
+    for copy in pass_copies:
+        copy.wait_recv()
     suf_copies = []
     for k in range(2):
         copy = remote(suf.at[2], suf.at[k], suf_s.at[k], suf_r.at[k], after[k])
         copy.start()
         suf_copies.append(copy)
-    suffix_ref[...] = jnp.where(lax.rem(m, 2) == 0, key_rows, value_rows)
-
-    for b in range(2):
-        vt[b] = cache_ref[pl.ds(b * 256, 256), pl.ds(HEAD, HEAD)].T
-
-    def block_of(j):
-        yy = lax.rem(y + lax.div(j, 2), 4)
-        cc = lax.rem(c + lax.rem(j, 2), 2)
-        return yy * 2 + cc, yy * 4 + zh * 2 + cc
-
-    def attend(block, tokens, cache, first):
-        queries = q_all[block]
-        pre = prefix_rows[pl.ds(tokens, 1), :]
-        return slot_part(
-            [cache[pl.ds(b * 256, 256), pl.ds(0, HEAD)] for b in range(2)],
-            [vt[first + b] for b in range(2)],
-            queries,
-            [pre == slot_prefix[first + b] for b in range(2)],
-        )
-
-    def first_half(j, carry):
-        block, tokens = block_of(j)
-
-        @pl.when(j > 0)
-        def _():
-            remote(q_all.at[block], q_all.at[block], q_s.at[0], q_r.at[block], z_peer).wait_recv()
-
-        peak, total, out = attend(block, tokens, cache_ref, 0)
-        half_stat[j, pl.ds(0, 1), :] = peak
-        half_stat[j, pl.ds(1, 1), :] = total
-        half_out[j] = out
-        return carry
-
-    lax.fori_loop(0, 8, first_half, 0)
+
+    def send_back(k, core):
+        yy = lax.rem(y + k, 4)
+        block, dev = core * 4 + yy, at_seq(yy * 4 + zh * 2 + core)
+        remote(res_out.at[block], back_out.at[mine], o_s.at[block], o_r.at[mine], dev).start()
+        remote(res_stat.at[block], back_stat.at[mine], st_s.at[block], st_r.at[mine], dev).start()
+
+    for core in range(2):
+        peak1, total1, out1 = attend(core, 2)
+        peak0 = half_stat[core, pl.ds(0, 1), :]
+        total0 = half_stat[core, pl.ds(1, 1), :]
+        peak = jnp.maximum(peak0, peak1)
+        f0, f1 = jnp.exp2(peak0 - peak), jnp.exp2(peak1 - peak)
+        total = total0 * f0 + total1 * f1
+        inverse = 1.0 / jnp.maximum(total, 1.0)
+        out = (half_out[core] * (f0 * inverse) + out1 * (f1 * inverse)).astype(BF16)
+        for yy in range(4):
+            cols = slice(yy * TOK, (yy + 1) * TOK)
+            res_out[core * 4 + yy] = out[:, cols]
+            res_stat[core * 4 + yy, pl.ds(0, 1), :] = peak[:, cols]
+            res_stat[core * 4 + yy, pl.ds(1, 1), :] = total[:, cols]
+        for k in (2, 1, 3):
+            send_back(k, core)
+        pl.when(c != core)(functools.partial(send_back, 0, core))
 
     for copy in suf_copies:
         copy.wait_recv()
@@ -286,39 +318,6 @@
         weight = jnp.exp2(suffix_scores[k] - suffix_peak)
         suffix_total += jnp.sum(weight, axis=0, keepdims=True)
         suffix_out += dot(suf[k, 1], weight.astype(BF16), 1, 0)
-
-    for copy in kv_copies:
-        copy.wait_recv()
-    for b in range(2):
-        vt[2 + b] = peer_cache[pl.ds(b * 256, 256), pl.ds(HEAD, HEAD)].T
-
-    def second_half(i, carry):
-        j = 7 - i
-        block, tokens = block_of(j)
-        peak1, total1, out1 = attend(block, tokens, peer_cache, 2)
-        peak0 = half_stat[j, pl.ds(0, 1), :]
-        total0 = half_stat[j, pl.ds(1, 1), :]
-        peak = jnp.maximum(peak0, peak1)
-        f0, f1 = jnp.exp2(peak0 - peak), jnp.exp2(peak1 - peak)
-        total = total0 * f0 + total1 * f1
-        inverse = 1.0 / jnp.maximum(total, 1.0)
-        res_out[block] = (half_out[j] * (f0 * inverse) + out1 * (f1 * inverse)).astype(BF16)
-        res_stat[block, pl.ds(0, 1), :] = peak
-        res_stat[block, pl.ds(1, 1), :] = total
-
-        @pl.when(j > 0)
-        def _():
-            dev = at_seq(tokens)
-            remote(
-                res_out.at[block], back_out.at[mine], o_s.at[block], o_r.at[mine], dev
-            ).start()
-            remote(
-                res_stat.at[block], back_stat.at[mine], st_s.at[block], st_r.at[mine], dev
-            ).start()
-
-        return carry
-
-    lax.fori_loop(0, 8, second_half, 0)
 
     parts = [(suffix_peak, suffix_total, suffix_out / suffix_total)]
     parts.append((res_stat[mine, pl.ds(0, 1), :], res_stat[mine, pl.ds(1, 1), :], res_out[mine]))
@@ -431,7 +430,7 @@
     )
     out_ref[...] = (residual.astype(F32) + summed).astype(BF16)
 
-    for copy in kv_copies + suf_copies + q_copies + sends1 + sends2 + g_copies:
+    for copy in kv_copies + pass_copies + suf_copies + q_copies + sends1 + sends2 + g_copies:
         copy.wait_send()
     for block, dev in yc_peers:
         remote(res_out.at[block], back_out.at[block], o_s.at[block], o_r.at[block], dev).wait_send()
@@ -473,6 +472,9 @@
     sine = jnp.concatenate([-sine, sine], axis=1)
     cache = lax.dynamic_slice_in_dim(prefix_slot_cache, my_model // 2, 1, 2).reshape(512, 2 * HEAD)
 
+    def in_hbm(value):
+        return pltpu.with_memory_space_constraint(value, pltpu.HBM)
+
     vmem = pl.BlockSpec(memory_space=pltpu.VMEM)
     smem = pl.BlockSpec(memory_space=pltpu.SMEM)
     hbm = pl.BlockSpec(memory_space=pl.ANY)
@@ -498,17 +500,17 @@
             V((2048, 384), BF16),
             V((384, 2048), BF16),
             V((128, 2048), BF16),
-            V((512, 256), BF16),
+            V((4, 256, 128), BF16),
             V((4, 128, 256), BF16),
             V((8,) + block, BF16),
             V((3, 2) + block, BF16),
-            V((8,) + block, F32),
-            V((8, 8, 128), F32),
+            V((2, 128, 512), F32),
+            V((2, 8, 512), F32),
             V((8,) + block, BF16),
             V((8, 8, 128), F32),
             V((8,) + block, BF16),
             V((8, 8, 128), F32),
-            V((16, 128), jnp.int32),
+            V((8, 512), jnp.int32),
             V((4, 4) + block, BF16),
             V((4, 3) + block, BF16),
             V((3,) + block, BF16),
@@ -519,6 +521,8 @@
             V((3,) + block, BF16),
             V((16,) + block, BF16),
             D((9,)),
+            D((2,)),
+            D((2,)),
             D((2,)),
             D((2,)),
             D((2,)),
@@ -548,20 +552,20 @@
         block_table,
         request_prefix,
         suffix_lengths,
-        hidden_in,
-        input_gain.reshape(1, -1),
-        post_gain.reshape(1, -1),
+        in_hbm(hidden_in),
+        in_hbm(input_gain.reshape(1, -1)),
+        in_hbm(post_gain.reshape(1, -1)),
         query_gain.reshape(1, -1),
         key_gain.reshape(1, -1),
         cosine,
         sine,
         cache,
-        w_query,
-        key_value_weight,
-        w_out,
-        w_gate,
-        w_up,
-        w_down,
+        in_hbm(w_query),
+        in_hbm(key_value_weight),
+        in_hbm(w_out),
+        in_hbm(w_gate),
+        in_hbm(w_up),
+        in_hbm(w_down),
     )
 
 

time: 78.2 us -> 68.5 us (0.88)
  Pallas kernels: 68.1 us -> 63.5 us
  local copies, waits for them, and re-layouts: 7.96 us -> 3.45 us
    pallas_call x1, Pallas kernels: 68.1 us -> 63.5 us  [local(): pl.pallas_call(kernel, out_shape=(jax.ShapeDtypeStruct((TOK, HEAD), BF16)...]
    unnamed x29 -> x15, local copies, waits for them, and re-layouts: 7.32 us -> 2.81 us
where the time goes in v2:
time: 68.5 us; the launch traced here: 68.4 us
  Pallas kernels  63.5 us (93%)
  local copies, waits for them, and re-layouts  3.45 us (5%)
  between operations  0.8 us (1%)
  other arithmetic  0.7 us (1%)
    pallas_call x1, Pallas kernels, local(): pl.pallas_call(kernel, out_shape=(jax.ShapeDtypeStruct((TOK, HEAD), BF16)...  63.5 us
    unnamed x15, local copies, waits for them, and re-layouts  2.81 us

profile of v2, /device:TPU:2, one launch (start us, length us, event | category | flops | bytes accessed | tf_op | source)
XLA Modules:
  0.0 68.4 jit_solution(17497889587494194056)
XLA Ops:
  0.6 0.0 copy-start
  0.6 0.0 copy-start.1
  0.7 0.0 copy-start.4
  0.7 0.0 copy-start.5
  0.7 0.0 copy-start.2
  0.7 0.0 copy-start.3
  0.7 1.5 %copy-done = bf16[2,256,8,256]{3,2,1,0:T(8,128)(2,1)S(1)} copy-done((bf16[2,256,8,256]{3,2,1,0:T(8,128)(2,1)S(1)}, bf16[2,256,8,256]{3,2,1,0:T(8,128)(2,1)}, u32[]{:S(2)}) %copy-start) | copy-done | bytes 2097176
  2.2 0.5 constant_dynamic-slice_fusion
  2.8 0.0 copy-done.1
  2.9 0.1 copy.20
  2.9 0.1 reduce-window.8
  3.0 0.1 reduce
  3.1 0.1 select_reduce_fusion
  3.2 0.3 fusion
  3.6 0.1 pad_maximum_fusion
  3.7 0.0 copy-done.4
  3.7 0.0 copy-done.5
  3.7 0.0 copy-done.2
  3.7 0.0 copy-done.3
  3.7 63.5 %layer.1 = (bf16[128,128]{1,0:T(8,128)(2,1)S(1)}, bf16[128,128]{1,0:T(8,128)(2,1)S(1)}) custom-call(s32[32]{0:T(128)S(1)} %copy-done.2, s32[32]{0:T(128)S(1)} %copy-done.3, s32[32]{0:T(128)S(1)} %copy-done.1, bf16[128,2048]{1,0:T(8,128)(2,1)} %hidden_hbm.1, f32[1,2048]{1,0:T(1,128)} %bitcast.10, f32[1,2048]{1,0:T(1,128)} %bitcast.11, f32[1,128]{1,0:T(1,128)S(1)} %bitcast.8, ...), custom_call_target="tpu_custom_call" | custom-call | tf_op jit(solution)/shard_map/layer/pallas_call | solution.py:484
  67.2 0.6 copy.25
  67.8 0.6 copy.26
  (5 shorter events, 0.1 us)
Async XLA Ops:
  0.6 1.6 %copy-start = (bf16[2,256,8,256]{3,2,1,0:T(8,128)(2,1)S(1)}, bf16[2,256,8,256]{3,2,1,0:T(8,128)(2,1)}, u32[]{:S(2)}) copy-start(bf16[2,256,8,256]{3,2,1,0:T(8,128)(2,1)} %param.26) | copy-start | bytes 6291460
  0.6 2.2 %copy-start.1 = (s32[32]{0:T(128)S(1)}, s32[32]{0:T(128)}, u32[]{:S(2)}) copy-start(s32[32]{0:T(128)} %lengths_ref.1) | copy-start | bytes 388
  0.7 3.0 %copy-start.4 = (f32[128]{0:T(128)S(1)}, f32[128]{0:T(128)}, u32[]{:S(2)}) copy-start(f32[128]{0:T(128)} %param.19) | copy-start | bytes 1540
  0.7 3.0 %copy-start.5 = (f32[128]{0:T(128)S(1)}, f32[128]{0:T(128)}, u32[]{:S(2)}) copy-start(f32[128]{0:T(128)} %param.20) | copy-start | bytes 1540
  0.7 3.0 %copy-start.2 = (s32[32]{0:T(128)S(1)}, s32[32]{0:T(128)}, u32[]{:S(2)}) copy-start(s32[32]{0:T(128)} %table_ref.1) | copy-start | bytes 388
  0.7 3.0 %copy-start.3 = (s32[32]{0:T(128)S(1)}, s32[32]{0:T(128)}, u32[]{:S(2)}) copy-start(s32[32]{0:T(128)} %request_prefix_ref.1) | copy-start | bytes 388

commit v3 on v2

--- a/solution.py
+++ b/solution.py
@@ -60,8 +60,6 @@
     post_gain_hbm,
     q_gain_ref,
     k_gain_ref,
-    cos_ref,
-    sin_ref,
     cache_ref,
     wq_hbm,
     wkv_hbm,
@@ -124,6 +122,7 @@
     z2_r,
     g_s,
     g_r,
+    ready,
 ):
     s = lax.axis_index("seq")
     m = lax.axis_index("mp")
@@ -159,25 +158,59 @@
     for dy, dc in ((0, 1), (1, 0), (1, 1), (3, 0), (3, 1), (2, 0), (2, 1)):
         yy, cc = lax.rem(y + dy, 4), lax.rem(c + dc, 2)
         yc_peers.append((cc * 4 + yy, at_seq(yy * 4 + zh * 2 + cc)))
+    mate = yc_peers[0][1]
+    y_peers = [yc_peers[k] for k in (5, 1, 3)]
     mine = c * 4 + y
     px = lax.rem(x, 2)
     x_partner = at_mp(zl * 4 + x + 1 - 2 * px)
-    after = [at_seq(lax.rem(s + 2, SEQ)), at_seq(lax.rem(s + 1, SEQ))]
-    before = [at_seq(lax.rem(s + 14, SEQ)), at_seq(lax.rem(s + 15, SEQ))]
+    after, before = at_seq(lax.rem(s + 2, SEQ)), at_seq(lax.rem(s + 14, SEQ))
     hops = (2, 1, 3)
     x_peers = [at_mp(zl * 4 + lax.rem(x + i, 4)) for i in hops]
     z_peers = [at_mp(lax.rem(zl + i, 4) * 4 + x) for i in hops]
 
+    same = [z_peer, after, before] + x_peers + z_peers + [dev for _, dev in y_peers]
     barrier = pltpu.get_barrier_semaphore()
-    everyone = [z_peer] + [p for _, p in yc_peers] + after + before + x_peers + z_peers
-    for dev in everyone:
+    for dev in same:
         pl.semaphore_signal(barrier, inc=1, device_id=dev, device_id_type=MESH)
+
+    @pl.when(c == 0)
+    def _():
+        pl.semaphore_signal(barrier, inc=1, device_id=mate, device_id_type=MESH)
+
+    def turn_values(slot):
+        vt[slot] = cache_ref[pl.ds(pl.multiple_of(slot * 256, 256), 256), pl.ds(HEAD, HEAD)].T
+
+    turn_values(px)
+    pl.semaphore_wait(barrier, len(same) + c)
+
+    @pl.when(c == 1)
+    def _():
+        pl.semaphore_signal(ready, inc=1, device_id=mate, device_id_type=MESH)
+
+    px_rows = pl.ds(pl.multiple_of(px * 256, 256), 256)
+    kv_copies = [
+        remote(
+            cache_ref.at[px_rows, pl.ds(0, HEAD)], kk.at[2 + px], kv_s.at[0], kv_r.at[0], z_peer
+        ),
+        remote(vt.at[px], vt.at[2 + px], kv_s.at[1], kv_r.at[1], z_peer),
+    ]
+    for copy in kv_copies:
+        copy.start()
+    turn_values(1 - px)
+
+    loads[0].wait()
+    loads[1].wait()
+    raw = hidden[...].astype(F32)
+    normed[...] = (raw * row_scale(raw) * gain[...]).astype(BF16)
 
     lane = lax.broadcasted_iota(jnp.int32, (8, 512), 1)
     core = lax.broadcasted_iota(jnp.int32, (8, 512), 0)
     block_at = lax.shift_right_logical(lane, 7) * 4 + zh * 2 + core
     token = block_at * TOK + (lane & 127)
     own_token = s * TOK + lax.broadcasted_iota(jnp.int32, (1, TOK), 1)
+    turn_lane = lax.broadcasted_iota(jnp.int32, (64, TOK), 1)
+    turn_token = s * TOK + lax.broadcasted_iota(jnp.int32, (64, TOK), 0) + (turn_lane & 64)
+    turn_start = jnp.zeros((64, TOK), jnp.int32)
     prefix = jnp.zeros((8, 512), jnp.int32)
     own_start = jnp.zeros((1, TOK), jnp.int32)
     begin = jnp.int32(0)
@@ -185,6 +218,7 @@
         end = begin + lengths_ref[r]
         prefix = jnp.where((token >= begin) & (token < end), request_prefix_ref[r], prefix)
         own_start = jnp.where((own_token >= begin) & (own_token < end), begin, own_start)
+        turn_start = jnp.where((turn_token >= begin) & (turn_token < end), begin, turn_start)
         begin = end
     prefix_rows[...] = prefix
 
@@ -196,25 +230,19 @@
             jnp.where(held == slot, jnp.int32(i // 8), p) for slot, p in zip(slot_ids, slot_prefix)
         ]
 
-    loads[0].wait()
-    loads[1].wait()
-    raw = hidden[...].astype(F32)
-    normed[...] = (raw * row_scale(raw) * gain[...]).astype(BF16)
-
-    for b in range(2):
-        kk[b] = cache_ref[pl.ds(b * 256, 256), pl.ds(0, HEAD)]
-        vt[b] = cache_ref[pl.ds(b * 256, 256), pl.ds(HEAD, HEAD)].T
-
-    pl.semaphore_wait(barrier, len(everyone))
-
-    kv_copies = [
-        remote(ref.at[px], ref.at[2 + px], kv_s.at[b], kv_r.at[b], z_peer)
-        for b, ref in enumerate((kk, vt))
-    ]
-    for copy in kv_copies:
-        copy.start()
-
-    cosine, sine = cos_ref[...], sin_ref[...]
+    inverse = jnp.exp((turn_lane & 63).astype(F32) * (-2.0 * math.log(THETA) / HEAD))
+    angles = (2048 + turn_token - turn_start).astype(F32) * inverse
+    lower = turn_lane < 64
+
+    def spread(packed):
+        other = pltpu.roll(packed, HEAD // 2, 1)
+        return jnp.concatenate(
+            [jnp.where(lower, packed, other), jnp.where(lower, other, packed)], axis=0
+        )
+
+    cosine, sine = spread(jnp.cos(angles)), spread(jnp.sin(angles))
+    half_lane = lax.broadcasted_iota(jnp.int32, (TOK, HEAD), 1)
+    sine = jnp.where(half_lane < HEAD // 2, -sine, sine)
 
     def head_rope(values, g):
         scaled = values * row_scale(values) * g
@@ -224,10 +252,14 @@
     q_raw = dot(normed[...], wq[...], 1, 0)
     q_all[mine] = head_rope(q_raw, q_gain_ref[...])
     q_copies = []
-    for k, (_, dev) in enumerate(yc_peers):
-        copy = remote(q_all.at[mine], q_all.at[mine], q_s.at[k], q_r.at[mine], dev)
+
+    def send_queries(n, block, dev):
+        copy = remote(q_all.at[block], q_all.at[block], q_s.at[n], q_r.at[block], dev)
         copy.start()
         q_copies.append(copy)
+
+    for n, (_, dev) in enumerate(y_peers):
+        send_queries(n, mine, dev)
 
     loads[3].wait()
     pair = dot(normed[...], wkv[...], 1, 0).astype(BF16)
@@ -237,6 +269,19 @@
     suf[2, 1] = value_rows.T
     suffix_ref[...] = jnp.where(lax.rem(m, 2) == 0, key_rows, value_rows)
 
+    suf_copy = remote(suf.at[2], suf.at[0], suf_s.at[0], suf_r.at[0], after)
+    suf_copy.start()
+
+    @pl.when(c == 0)
+    def _():
+        pl.semaphore_wait(ready, 1)
+        remote(suf.at[2], suf.at[1], suf_s.at[1], suf_r.at[1], mate).start()
+
+    send_queries(3, mine, mate)
+    for n, (block, dev) in enumerate(y_peers):
+        remote(q_all.at[block], q_all.at[block], q_s.at[0], q_r.at[block], dev).wait_recv()
+        send_queries(4 + n, block, mate)
+
     pass_copies = []
     for b, ref in enumerate((kk, vt)):
         kv_copies[b].wait_recv()
@@ -244,34 +289,35 @@
         copy.start()
         pass_copies.append(copy)
 
-    def attend(core, first):
+    def attend(core, first, keys):
         return slot_part(
-            [kk[first + b] for b in range(2)],
+            keys,
             [vt[first + b] for b in range(2)],
             q_all[pl.ds(core * 4, 4)].reshape(512, HEAD),
             [prefix_rows[pl.ds(core, 1), :] == slot_prefix[first + b] for b in range(2)],
         )
 
-    def q_arrived(k, core):
-        block = core * 4 + lax.rem(y + k, 4)
-        remote(q_all.at[block], q_all.at[block], q_s.at[0], q_r.at[block], z_peer).wait_recv()
+    own_keys = [cache_ref[pl.ds(b * 256, 256), pl.ds(0, HEAD)] for b in range(2)]
+
+    def q_arrived(core):
+        for k in range(4):
+            block = core * 4 + k
+            remote(q_all.at[block], q_all.at[block], q_s.at[0], q_r.at[block], mate).wait_recv()
 
     for core in range(2):
-        for k in (1, 3, 2):
-            q_arrived(k, core)
-        pl.when(c != core)(functools.partial(q_arrived, 0, core))
-        peak, total, out = attend(core, 0)
+        pl.when(c != core)(functools.partial(q_arrived, core))
+        peak, total, out = attend(core, 0, own_keys)
         half_stat[core, pl.ds(0, 1), :] = peak
         half_stat[core, pl.ds(1, 1), :] = total
         half_out[core] = out
 
     for copy in pass_copies:
         copy.wait_recv()
-    suf_copies = []
-    for k in range(2):
-        copy = remote(suf.at[2], suf.at[k], suf_s.at[k], suf_r.at[k], after[k])
-        copy.start()
-        suf_copies.append(copy)
+    suf_copy.wait_recv()
+
+    @pl.when(c == 1)
+    def _():
+        remote(suf.at[0], suf.at[1], suf_s.at[1], suf_r.at[1], mate).start()
 
     def send_back(k, core):
         yy = lax.rem(y + k, 4)
@@ -280,7 +326,7 @@
         remote(res_stat.at[block], back_stat.at[mine], st_s.at[block], st_r.at[mine], dev).start()
 
     for core in range(2):
-        peak1, total1, out1 = attend(core, 2)
+        peak1, total1, out1 = attend(core, 2, [kk[2], kk[3]])
         peak0 = half_stat[core, pl.ds(0, 1), :]
         total0 = half_stat[core, pl.ds(1, 1), :]
         peak = jnp.maximum(peak0, peak1)
@@ -297,8 +343,7 @@
             send_back(k, core)
         pl.when(c != core)(functools.partial(send_back, 0, core))
 
-    for copy in suf_copies:
-        copy.wait_recv()
+    remote(suf.at[0], suf.at[1], suf_s.at[1], suf_r.at[1], mate).wait_recv()
     queries = q_all[mine]
     suffix_scores = []
     for k in range(3):
@@ -430,7 +475,8 @@
     )
     out_ref[...] = (residual.astype(F32) + summed).astype(BF16)
 
-    for copy in kv_copies + pass_copies + suf_copies + q_copies + sends1 + sends2 + g_copies:
+    remote(suf.at[2], suf.at[1], suf_s.at[1], suf_r.at[1], mate).wait_send()
+    for copy in kv_copies + pass_copies + [suf_copy] + q_copies + sends1 + sends2 + g_copies:
         copy.wait_send()
     for block, dev in yc_peers:
         remote(res_out.at[block], back_out.at[block], o_s.at[block], o_r.at[block], dev).wait_send()
@@ -456,21 +502,8 @@
     request_prefix,
     suffix_lengths,
 ):
-    my_seq = lax.axis_index("seq")
     my_model = lax.axis_index("mp")
-    own = my_seq * TOK + jnp.arange(TOK, dtype=jnp.int32)
-    ends = jnp.cumsum(suffix_lengths)
-    starts = ends - suffix_lengths
-    inside = (own[:, None] >= starts[None, :]) & (own[:, None] < ends[None, :])
-    start_of = jnp.sum(inside.astype(jnp.int32) * starts[None, :], axis=1)
-    rotary_pos = (2048 + own - start_of).astype(F32)
-    half = HEAD // 2
-    inverse = jnp.exp(jnp.arange(half).astype(F32) * (-2.0 * math.log(THETA) / HEAD))
-    angles = rotary_pos[:, None] * inverse[None, :]
-    cosine, sine = jnp.cos(angles), jnp.sin(angles)
-    cosine = jnp.concatenate([cosine, cosine], axis=1)
-    sine = jnp.concatenate([-sine, sine], axis=1)
-    cache = lax.dynamic_slice_in_dim(prefix_slot_cache, my_model // 2, 1, 2).reshape(512, 2 * HEAD)
+    cache = lax.dynamic_slice_in_dim(prefix_slot_cache, lax.div(my_model, 2), 1, 2).reshape(512, 2 * HEAD)
 
     def in_hbm(value):
         return pltpu.with_memory_space_constraint(value, pltpu.HBM)
@@ -487,7 +520,7 @@
             jax.ShapeDtypeStruct((TOK, HEAD), BF16),
             jax.ShapeDtypeStruct((TOK, HEAD), BF16),
         ),
-        in_specs=[smem] * 3 + [hbm] * 3 + [vmem] * 5 + [hbm] * 6,
+        in_specs=[smem] * 3 + [hbm] * 3 + [vmem] * 3 + [hbm] * 6,
         out_specs=(vmem, vmem),
         scratch_shapes=[
             V((128, 2048), BF16),
@@ -543,6 +576,7 @@
             D((3,)),
             D((15,)),
             D((16,)),
+            pltpu.SemaphoreType.REGULAR,
         ],
         compiler_params=pltpu.CompilerParams(
             collective_id=0, has_side_effects=True, vmem_limit_bytes=48 * 1024 * 1024
@@ -557,8 +591,6 @@
         in_hbm(post_gain.reshape(1, -1)),
         query_gain.reshape(1, -1),
         key_gain.reshape(1, -1),
-        cosine,
-        sine,
         cache,
         in_hbm(w_query),
         in_hbm(key_value_weight),

time: 68.5 us -> 63.1 us (0.921)
  Pallas kernels: 63.5 us -> 58.9 us
  other arithmetic: 0.7 us -> 0 us
    pallas_call x1, Pallas kernels: 63.5 us -> 58.9 us  [local(): pl.pallas_call(kernel, out_shape=(jax.ShapeDtypeStruct((TOK, HEAD), BF16)...]
where the time goes in v3:
time: 63.1 us; the launch traced here: 63 us
  Pallas kernels  58.9 us (93%)
  local copies, waits for them, and re-layouts  3.37 us (5%)
  between operations  0.75 us (1%)
    pallas_call x1, Pallas kernels, local(): pl.pallas_call(kernel, out_shape=(jax.ShapeDtypeStruct((TOK, HEAD), BF16)...  58.9 us
    unnamed x15, local copies, waits for them, and re-layouts  2.82 us

profile of v3, /device:TPU:2, one launch (start us, length us, event | category | flops | bytes accessed | tf_op | source)
XLA Modules:
  0.0 63.0 jit_solution(15250822304013209851)
XLA Ops:
  0.6 0.0 copy-start
  0.6 0.0 copy-start.3
  0.7 0.0 copy-start.2
  0.7 0.0 copy-start.1
  0.7 0.0 copy-start.5
  0.7 0.0 copy-start.4
  0.7 1.5 %copy-done = bf16[2,256,8,256]{3,2,1,0:T(8,128)(2,1)S(1)} copy-done((bf16[2,256,8,256]{3,2,1,0:T(8,128)(2,1)S(1)}, bf16[2,256,8,256]{3,2,1,0:T(8,128)(2,1)}, u32[]{:S(2)}) %copy-start) | copy-done | bytes 2097176
  2.2 0.5 constant_dynamic-slice_fusion
  2.8 0.0 copy-done.3
  2.8 0.0 copy-done.2
  2.8 0.0 copy-done.1
  2.9 0.0 copy-done.5
  2.9 0.0 copy-done.4
  2.9 58.9 %layer.1 = (bf16[128,128]{1,0:T(8,128)(2,1)S(1)}, bf16[128,128]{1,0:T(8,128)(2,1)S(1)}) custom-call(s32[32]{0:T(128)S(1)} %copy-done.1, s32[32]{0:T(128)S(1)} %copy-done.2, s32[32]{0:T(128)S(1)} %copy-done.3, bf16[128,2048]{1,0:T(8,128)(2,1)} %hidden_hbm.1, f32[1,2048]{1,0:T(1,128)} %bitcast.8, f32[1,2048]{1,0:T(1,128)} %bitcast.9, f32[1,128]{1,0:T(1,128)S(1)} %bitcast.6, ...), custom_call_target="tpu_custom_call" | custom-call | tf_op jit(solution)/shard_map/layer/pallas_call | solution.py:517
  61.7 0.6 copy.21
  62.4 0.6 copy.22
  (1 shorter events, 0.0 us)
Async XLA Ops:
  0.6 1.6 %copy-start = (bf16[2,256,8,256]{3,2,1,0:T(8,128)(2,1)S(1)}, bf16[2,256,8,256]{3,2,1,0:T(8,128)(2,1)}, u32[]{:S(2)}) copy-start(bf16[2,256,8,256]{3,2,1,0:T(8,128)(2,1)} %param.26) | copy-start | bytes 6291460
  0.6 2.2 %copy-start.3 = (s32[32]{0:T(128)S(1)}, s32[32]{0:T(128)}, u32[]{:S(2)}) copy-start(s32[32]{0:T(128)} %lengths_ref.1) | copy-start | bytes 388
  0.7 2.2 %copy-start.2 = (s32[32]{0:T(128)S(1)}, s32[32]{0:T(128)}, u32[]{:S(2)}) copy-start(s32[32]{0:T(128)} %request_prefix_ref.1) | copy-start | bytes 388
  0.7 2.2 %copy-start.1 = (s32[32]{0:T(128)S(1)}, s32[32]{0:T(128)}, u32[]{:S(2)}) copy-start(s32[32]{0:T(128)} %table_ref.1) | copy-start | bytes 388
  0.7 2.2 %copy-start.5 = (f32[128]{0:T(128)S(1)}, f32[128]{0:T(128)}, u32[]{:S(2)}) copy-start(f32[128]{0:T(128)} %param.20) | copy-start | bytes 1540
  0.7 2.2 %copy-start.4 = (f32[128]{0:T(128)S(1)}, f32[128]{0:T(128)}, u32[]{:S(2)}) copy-start(f32[128]{0:T(128)} %param.19) | copy-start | bytes 1540

commit v4 on v3

--- a/solution.py
+++ b/solution.py
@@ -442,32 +442,36 @@
             gathered.at[block], gathered.at[block], g_s.at[0], g_r.at[block], z_peers[0]
         ).wait_recv()
 
-    for dev in z_peers:
-        share(m, dev)
+    z_rows = [zl, zl + 1 - 2 * lax.rem(zl, 2), lax.rem(zl + 2, 4), 3 - zl]
+    for i in (3, 2, 1):
+        share(m, at_mp(z_rows[i] * 4 + x))
     for dev in x_peers:
         share(m, dev)
-    for i in (1, 3, 2):
-        block = lax.rem(zl + i, 4) * 4 + x
-        arrived(block)
+    for i in (1, 2, 3):
+        arrived(z_rows[i] * 4 + x)
         for dev in x_peers:
-            share(block, dev)
-    for i in (1, 3, 2):
-        for zz in range(4):
-            arrived(zz * 4 + lax.rem(x + i, 4))
-
+            share(z_rows[i] * 4 + x, dev)
+    for k in (5, 6, 7):
+        loads[k].wait()
     square = jnp.zeros((TOK, HEAD), F32)
-    for k in range(16):
-        v = gathered[k].astype(F32)
-        square = square + v * v
+    gate, up = None, None
+    for i in range(4):
+        for hop in (1, 3, 2):
+            arrived(z_rows[i] * 4 + lax.rem(x + hop, 4))
+        base = z_rows[i] * 4
+        scaled = []
+        for k in range(4):
+            v = gathered[base + k].astype(F32)
+            square = square + v * v
+            cols = pl.ds(pl.multiple_of((base + k) * HEAD, HEAD), HEAD)
+            scaled.append((v * post_gain[:, cols]).astype(BF16))
+        scaled = jnp.concatenate(scaled, axis=1)
+        rows = pl.ds(pl.multiple_of(base * HEAD, 4 * HEAD), 4 * HEAD)
+        gate_part, up_part = dot(scaled, wg[rows, :], 1, 0), dot(scaled, wu[rows, :], 1, 0)
+        gate = gate_part if gate is None else gate + gate_part
+        up = up_part if up is None else up + up_part
     scale = lax.rsqrt(jnp.sum(square, axis=-1, keepdims=True) * (1.0 / 2048) + EPSILON)
-    loads[5].wait()
-    for k in range(16):
-        cols = pl.ds(k * HEAD, HEAD)
-        normed[:, cols] = (gathered[k].astype(F32) * scale * post_gain[:, cols]).astype(BF16)
-    loads[6].wait()
-    gate = dot(normed[...], wg[...], 1, 0)
-    loads[7].wait()
-    up = dot(normed[...], wu[...], 1, 0)
+    gate, up = gate * scale, up * scale
     middle = (gate / (1.0 + jnp.exp(-gate)) * up).astype(BF16)
     loads[8].wait()
     summed, sends2 = reduce_scatter(

time: 63.1 us -> 61.7 us (0.978)
  Pallas kernels: 58.9 us -> 57.3 us
    pallas_call x1, Pallas kernels: 58.9 us -> 57.3 us  [local(): pl.pallas_call(kernel, out_shape=(jax.ShapeDtypeStruct((TOK, HEAD), BF16)...]
where the time goes in v4:
time: 61.7 us; the launch traced here: 61.4 us
  Pallas kernels  57.3 us (93%)
  local copies, waits for them, and re-layouts  3.37 us (5%)
  between operations  0.75 us (1%)
    pallas_call x1, Pallas kernels, local(): pl.pallas_call(kernel, out_shape=(jax.ShapeDtypeStruct((TOK, HEAD), BF16)...  57.3 us
    unnamed x15, local copies, waits for them, and re-layouts  2.82 us

profile of v4, /device:TPU:2, one launch (start us, length us, event | category | flops | bytes accessed | tf_op | source)
XLA Modules:
  0.0 61.4 jit_solution(13296568511018394060)
XLA Ops:
  0.6 0.0 copy-start
  0.6 0.0 copy-start.3
  0.7 0.0 copy-start.2
  0.7 0.0 copy-start.1
  0.7 0.0 copy-start.5
  0.7 0.0 copy-start.4
  0.7 1.5 %copy-done = bf16[2,256,8,256]{3,2,1,0:T(8,128)(2,1)S(1)} copy-done((bf16[2,256,8,256]{3,2,1,0:T(8,128)(2,1)S(1)}, bf16[2,256,8,256]{3,2,1,0:T(8,128)(2,1)}, u32[]{:S(2)}) %copy-start) | copy-done | bytes 2097176
  2.2 0.5 constant_dynamic-slice_fusion
  2.8 0.0 copy-done.3
  2.8 0.0 copy-done.2
  2.8 0.0 copy-done.1
  2.9 0.0 copy-done.5
  2.9 0.0 copy-done.4
  2.9 57.3 %layer.1 = (bf16[128,128]{1,0:T(8,128)(2,1)S(1)}, bf16[128,128]{1,0:T(8,128)(2,1)S(1)}) custom-call(s32[32]{0:T(128)S(1)} %copy-done.1, s32[32]{0:T(128)S(1)} %copy-done.2, s32[32]{0:T(128)S(1)} %copy-done.3, bf16[128,2048]{1,0:T(8,128)(2,1)} %hidden_hbm.1, f32[1,2048]{1,0:T(1,128)} %bitcast.8, f32[1,2048]{1,0:T(1,128)} %bitcast.9, f32[1,128]{1,0:T(1,128)S(1)} %bitcast.6, ...), custom_call_target="tpu_custom_call" | custom-call | tf_op jit(solution)/shard_map/layer/pallas_call | solution.py:521
  60.1 0.6 %copy.21 = bf16[128,128]{1,0:T(8,128)(2,1)} copy(bf16[128,128]{1,0:T(8,128)(2,1)S(1)} %get-tuple-element.4) | data formatting | bytes 65536
  60.8 0.6 %copy.22 = bf16[128,128]{1,0:T(8,128)(2,1)} copy(bf16[128,128]{1,0:T(8,128)(2,1)S(1)} %get-tuple-element.5) | data formatting | bytes 65536
  (1 shorter events, 0.0 us)
Async XLA Ops:
  0.6 1.6 %copy-start = (bf16[2,256,8,256]{3,2,1,0:T(8,128)(2,1)S(1)}, bf16[2,256,8,256]{3,2,1,0:T(8,128)(2,1)}, u32[]{:S(2)}) copy-start(bf16[2,256,8,256]{3,2,1,0:T(8,128)(2,1)} %param.26) | copy-start | bytes 6291460
  0.6 2.2 %copy-start.3 = (s32[32]{0:T(128)S(1)}, s32[32]{0:T(128)}, u32[]{:S(2)}) copy-start(s32[32]{0:T(128)} %lengths_ref.1) | copy-start | bytes 388
  0.7 2.2 %copy-start.2 = (s32[32]{0:T(128)S(1)}, s32[32]{0:T(128)}, u32[]{:S(2)}) copy-start(s32[32]{0:T(128)} %request_prefix_ref.1) | copy-start | bytes 388
  0.7 2.2 %copy-start.1 = (s32[32]{0:T(128)S(1)}, s32[32]{0:T(128)}, u32[]{:S(2)}) copy-start(s32[32]{0:T(128)} %table_ref.1) | copy-start | bytes 388
  0.7 2.2 %copy-start.5 = (f32[128]{0:T(128)S(1)}, f32[128]{0:T(128)}, u32[]{:S(2)}) copy-start(f32[128]{0:T(128)} %param.20) | copy-start | bytes 1540
  0.7 2.2 %copy-start.4 = (f32[128]{0:T(128)S(1)}, f32[128]{0:T(128)}, u32[]{:S(2)}) copy-start(f32[128]{0:T(128)} %param.19) | copy-start | bytes 1540

commit v5 on v4

--- a/solution.py
+++ b/solution.py
@@ -68,7 +68,6 @@
     wu_hbm,
     wd_hbm,
     out_ref,
-    suffix_ref,
     hidden,
     gain,
     post_gain,
@@ -267,7 +266,7 @@
     value_rows = pair[:, HEAD:]
     suf[2, 0] = key_rows
     suf[2, 1] = value_rows.T
-    suffix_ref[...] = jnp.where(lax.rem(m, 2) == 0, key_rows, value_rows)
+    out_ref[1] = jnp.where(lax.rem(m, 2) == 0, key_rows, value_rows)
 
     suf_copy = remote(suf.at[2], suf.at[0], suf_s.at[0], suf_r.at[0], after)
     suf_copy.start()
@@ -386,10 +385,11 @@
     attended = (accumulated / weight_sum).astype(BF16)
     attended = attended.T
 
+    z_rows = [zl, zl + 1 - 2 * lax.rem(zl, 2), lax.rem(zl + 2, 4), 3 - zl]
     def reduce_scatter(left, weight, blocks, from_x, from_z, to_z, xs, xr, zs, zr):
         sends = []
-        for i in (2, 1, 3, 0):
-            zz = lax.rem(zl + i, 4)
+        for i in (3, 2, 1, 0):
+            zz = z_rows[i]
             prod = dot(left, weight[:, pl.ds(pl.multiple_of(zz * 512, 512), 512)], 1, 0)
             prod = prod.astype(BF16)
             for k in range(4):
@@ -405,7 +405,7 @@
                 copy.start()
                 sends.append(copy)
         z_sends = []
-        for n, i in enumerate((2, 1, 3, 0)):
+        for n, i in enumerate((3, 2, 1, 0)):
             for k in range(3):
                 sends[n * 3 + k].wait_recv()
             acc = blocks[i, x].astype(F32)
@@ -413,7 +413,7 @@
                 acc = acc + from_x[i, k].astype(F32)
             if i:
                 to_z[n] = acc.astype(BF16)
-                copy = remote(to_z.at[n], from_z.at[n], zs.at[n], zr.at[n], z_peers[n])
+                copy = remote(to_z.at[n], from_z.at[n], zs.at[n], zr.at[n], at_mp(z_rows[i] * 4 + x))
                 copy.start()
                 z_sends.append(copy)
         for n, copy in enumerate(z_sends):
@@ -442,7 +442,6 @@
             gathered.at[block], gathered.at[block], g_s.at[0], g_r.at[block], z_peers[0]
         ).wait_recv()
 
-    z_rows = [zl, zl + 1 - 2 * lax.rem(zl, 2), lax.rem(zl + 2, 4), 3 - zl]
     for i in (3, 2, 1):
         share(m, at_mp(z_rows[i] * 4 + x))
     for dev in x_peers:
@@ -477,7 +476,7 @@
     summed, sends2 = reduce_scatter(
         middle, wd, part2, part2_x, part2_z, sent2_z, x2_s, x2_r, z2_s, z2_r
     )
-    out_ref[...] = (residual.astype(F32) + summed).astype(BF16)
+    out_ref[0] = (residual.astype(F32) + summed).astype(BF16)
 
     remote(suf.at[2], suf.at[1], suf_s.at[1], suf_r.at[1], mate).wait_send()
     for copy in kv_copies + pass_copies + [suf_copy] + q_copies + sends1 + sends2 + g_copies:
@@ -518,14 +517,11 @@
     V = pltpu.VMEM
     D = pltpu.SemaphoreType.DMA
     block = (TOK, HEAD)
-    return pl.pallas_call(
+    both = pl.pallas_call(
         kernel,
-        out_shape=(
-            jax.ShapeDtypeStruct((TOK, HEAD), BF16),
-            jax.ShapeDtypeStruct((TOK, HEAD), BF16),
-        ),
+        out_shape=jax.ShapeDtypeStruct((2, TOK, HEAD), BF16),
         in_specs=[smem] * 3 + [hbm] * 3 + [vmem] * 3 + [hbm] * 6,
-        out_specs=(vmem, vmem),
+        out_specs=vmem,
         scratch_shapes=[
             V((128, 2048), BF16),
             V((1, 2048), F32),
@@ -604,6 +600,8 @@
         in_hbm(w_down),
     )
 
+    return both[0], both[1]
+
 
 def solution(mesh):
     in_specs = (

time: 61.7 us -> 60.8 us (0.985)
    unnamed x15 -> x13, local copies, waits for them, and re-layouts: 2.82 us -> 1.59 us
    squeeze x0 -> x1, local copies, waits for them, and re-layouts: none -> 0.63 us  [local(): return (both[0], both[1])]
where the time goes in v5:
time: 60.8 us; the launch traced here: 60.5 us
  Pallas kernels  57 us (94%)
  local copies, waits for them, and re-layouts  2.77 us (5%)
  between operations  0.75 us (1%)
    pallas_call x1, Pallas kernels, local(): pl.pallas_call(kernel, out_shape=jax.ShapeDtypeStruct((2, TOK, HEAD), BF1...  57 us
    unnamed x13, local copies, waits for them, and re-layouts  1.59 us

profile of v5, /device:TPU:2, one launch (start us, length us, event | category | flops | bytes accessed | tf_op | source)
XLA Modules:
  0.0 60.5 jit_solution(13608261644288842463)
XLA Ops:
  0.6 0.0 copy-start
  0.6 0.0 copy-start.3
  0.7 0.0 copy-start.2
  0.7 0.0 copy-start.1
  0.7 0.0 copy-start.5
  0.7 0.0 copy-start.4
  0.7 1.5 %copy-done = bf16[2,256,8,256]{3,2,1,0:T(8,128)(2,1)S(1)} copy-done((bf16[2,256,8,256]{3,2,1,0:T(8,128)(2,1)S(1)}, bf16[2,256,8,256]{3,2,1,0:T(8,128)(2,1)}, u32[]{:S(2)}) %copy-start) | copy-done | bytes 2097176
  2.2 0.5 constant_dynamic-slice_fusion
  2.8 0.0 copy-done.3
  2.8 0.0 copy-done.2
  2.8 0.0 copy-done.1
  2.9 0.0 copy-done.5
  2.9 0.0 copy-done.4
  2.9 57.0 %layer.1 = bf16[2,128,128]{2,1,0:T(8,128)(2,1)S(1)} custom-call(s32[32]{0:T(128)S(1)} %copy-done.1, s32[32]{0:T(128)S(1)} %copy-done.2, s32[32]{0:T(128)S(1)} %copy-done.3, bf16[128,2048]{1,0:T(8,128)(2,1)} %hidden_hbm.1, f32[1,2048]{1,0:T(1,128)} %bitcast.12, f32[1,2048]{1,0:T(1,128)} %bitcast.13, f32[1,128]{1,0:T(1,128)S(1)} %bitcast.10, ...), custom_call_target="tpu_custom_call" | custom-call | tf_op jit(solution)/shard_map/layer/pallas_call | solution.py:520
  59.9 0.6 %slice_bitcast_fusion = (bf16[128,128]{1,0:T(8,128)(2,1)}, bf16[128,128]{1,0:T(8,128)(2,1)}) fusion(bf16[2,128,128]{2,1,0:T(8,128)(2,1)S(1)} %layer.1), kind=kLoop, calls=%fused_computation | loop fusion | bytes 131072 | tf_op jit(solution)/shard_map/squeeze | solution.py:603
  (1 shorter events, 0.0 us)
Async XLA Ops:
  0.6 1.6 %copy-start = (bf16[2,256,8,256]{3,2,1,0:T(8,128)(2,1)S(1)}, bf16[2,256,8,256]{3,2,1,0:T(8,128)(2,1)}, u32[]{:S(2)}) copy-start(bf16[2,256,8,256]{3,2,1,0:T(8,128)(2,1)} %param.26) | copy-start | bytes 6291460
  0.6 2.2 %copy-start.3 = (s32[32]{0:T(128)S(1)}, s32[32]{0:T(128)}, u32[]{:S(2)}) copy-start(s32[32]{0:T(128)} %lengths_ref.1) | copy-start | bytes 388
  0.7 2.2 %copy-start.2 = (s32[32]{0:T(128)S(1)}, s32[32]{0:T(128)}, u32[]{:S(2)}) copy-start(s32[32]{0:T(128)} %request_prefix_ref.1) | copy-start | bytes 388
  0.7 2.2 %copy-start.1 = (s32[32]{0:T(128)S(1)}, s32[32]{0:T(128)}, u32[]{:S(2)}) copy-start(s32[32]{0:T(128)} %table_ref.1) | copy-start | bytes 388
  0.7 2.2 %copy-start.5 = (f32[128]{0:T(128)S(1)}, f32[128]{0:T(128)}, u32[]{:S(2)}) copy-start(f32[128]{0:T(128)} %param.20) | copy-start | bytes 1540
  0.7 2.2 %copy-start.4 = (f32[128]{0:T(128)S(1)}, f32[128]{0:T(128)}, u32[]{:S(2)}) copy-start(f32[128]{0:T(128)} %param.19) | copy-start | bytes 1540

commit v6 on v5

--- a/solution.py
+++ b/solution.py
@@ -134,6 +134,30 @@
     def at_mp(i):
         return {"mp": i}
 
+    z_peer = at_seq(y * 4 + (1 - zh) * 2 + c)
+    yc_peers = []
+    for dy, dc in ((0, 1), (1, 0), (1, 1), (3, 0), (3, 1), (2, 0), (2, 1)):
+        yy, cc = lax.rem(y + dy, 4), lax.rem(c + dc, 2)
+        yc_peers.append((cc * 4 + yy, at_seq(yy * 4 + zh * 2 + cc)))
+    mate = yc_peers[0][1]
+    y_peers = [yc_peers[k] for k in (5, 1, 3)]
+    mine = c * 4 + y
+    px = lax.rem(x, 2)
+    x_partner = at_mp(zl * 4 + x + 1 - 2 * px)
+    after, before = at_seq(lax.rem(s + 2, SEQ)), at_seq(lax.rem(s + 14, SEQ))
+    hops = (2, 1, 3)
+    x_peers = [at_mp(zl * 4 + lax.rem(x + i, 4)) for i in hops]
+    z_peers = [at_mp(lax.rem(zl + i, 4) * 4 + x) for i in hops]
+
+    same = [z_peer, after, before] + x_peers + z_peers + [dev for _, dev in y_peers]
+    barrier = pltpu.get_barrier_semaphore()
+    for dev in same:
+        pl.semaphore_signal(barrier, inc=1, device_id=dev, device_id_type=MESH)
+
+    @pl.when(c == 0)
+    def _():
+        pl.semaphore_signal(barrier, inc=1, device_id=mate, device_id_type=MESH)
+
     loads = []
     for k, (src, dst) in enumerate(
         [
@@ -151,30 +175,6 @@
         copy = pltpu.make_async_copy(src, dst, dma_sem.at[k])
         copy.start()
         loads.append(copy)
-
-    z_peer = at_seq(y * 4 + (1 - zh) * 2 + c)
-    yc_peers = []
-    for dy, dc in ((0, 1), (1, 0), (1, 1), (3, 0), (3, 1), (2, 0), (2, 1)):
-        yy, cc = lax.rem(y + dy, 4), lax.rem(c + dc, 2)
-        yc_peers.append((cc * 4 + yy, at_seq(yy * 4 + zh * 2 + cc)))
-    mate = yc_peers[0][1]
-    y_peers = [yc_peers[k] for k in (5, 1, 3)]
-    mine = c * 4 + y
-    px = lax.rem(x, 2)
-    x_partner = at_mp(zl * 4 + x + 1 - 2 * px)
-    after, before = at_seq(lax.rem(s + 2, SEQ)), at_seq(lax.rem(s + 14, SEQ))
-    hops = (2, 1, 3)
-    x_peers = [at_mp(zl * 4 + lax.rem(x + i, 4)) for i in hops]
-    z_peers = [at_mp(lax.rem(zl + i, 4) * 4 + x) for i in hops]
-
-    same = [z_peer, after, before] + x_peers + z_peers + [dev for _, dev in y_peers]
-    barrier = pltpu.get_barrier_semaphore()
-    for dev in same:
-        pl.semaphore_signal(barrier, inc=1, device_id=dev, device_id_type=MESH)
-
-    @pl.when(c == 0)
-    def _():
-        pl.semaphore_signal(barrier, inc=1, device_id=mate, device_id_type=MESH)
 
     def turn_values(slot):
         vt[slot] = cache_ref[pl.ds(pl.multiple_of(slot * 256, 256), 256), pl.ds(HEAD, HEAD)].T
@@ -310,14 +310,14 @@
         half_stat[core, pl.ds(1, 1), :] = total
         half_out[core] = out
 
-    for copy in pass_copies:
-        copy.wait_recv()
     suf_copy.wait_recv()
 
     @pl.when(c == 1)
     def _():
         remote(suf.at[0], suf.at[1], suf_s.at[1], suf_r.at[1], mate).start()
 
+    for copy in pass_copies:
+        copy.wait_recv()
     def send_back(k, core):
         yy = lax.rem(y + k, 4)
         block, dev = core * 4 + yy, at_seq(yy * 4 + zh * 2 + core)
@@ -386,7 +386,19 @@
     attended = attended.T
 
     z_rows = [zl, zl + 1 - 2 * lax.rem(zl, 2), lax.rem(zl + 2, 4), 3 - zl]
-    def reduce_scatter(left, weight, blocks, from_x, from_z, to_z, xs, xr, zs, zr):
+    def drain_attention():
+        remote(suf.at[2], suf.at[1], suf_s.at[1], suf_r.at[1], mate).wait_send()
+        for copy in kv_copies + pass_copies + [suf_copy] + q_copies:
+            copy.wait_send()
+        for block, dev in yc_peers:
+            remote(
+                res_out.at[block], back_out.at[block], o_s.at[block], o_r.at[block], dev
+            ).wait_send()
+            remote(
+                res_stat.at[block], back_stat.at[block], st_s.at[block], st_r.at[block], dev
+            ).wait_send()
+
+    def reduce_scatter(left, weight, blocks, from_x, from_z, to_z, xs, xr, zs, zr, meanwhile):
         sends = []
         for i in (3, 2, 1, 0):
             zz = z_rows[i]
@@ -404,6 +416,7 @@
                 )
                 copy.start()
                 sends.append(copy)
+        meanwhile()
         z_sends = []
         for n, i in enumerate((3, 2, 1, 0)):
             for k in range(3):
@@ -423,7 +436,7 @@
 
     loads[4].wait()
     summed, sends1 = reduce_scatter(
-        attended, wo, part, part_x, part_z, sent_z, x_s, x_r, z_s, z_r
+        attended, wo, part, part_x, part_z, sent_z, x_s, x_r, z_s, z_r, drain_attention
     )
     columns = pl.ds(pl.multiple_of(m * HEAD, HEAD), HEAD)
     residual = (hidden[:, columns].astype(F32) + summed).astype(BF16)
@@ -472,20 +485,19 @@
     scale = lax.rsqrt(jnp.sum(square, axis=-1, keepdims=True) * (1.0 / 2048) + EPSILON)
     gate, up = gate * scale, up * scale
     middle = (gate / (1.0 + jnp.exp(-gate)) * up).astype(BF16)
+
+    def drain_residual():
+        for copy in sends1 + g_copies:
+            copy.wait_send()
+
     loads[8].wait()
     summed, sends2 = reduce_scatter(
-        middle, wd, part2, part2_x, part2_z, sent2_z, x2_s, x2_r, z2_s, z2_r
+        middle, wd, part2, part2_x, part2_z, sent2_z, x2_s, x2_r, z2_s, z2_r, drain_residual
     )
     out_ref[0] = (residual.astype(F32) + summed).astype(BF16)
 
-    remote(suf.at[2], suf.at[1], suf_s.at[1], suf_r.at[1], mate).wait_send()
-    for copy in kv_copies + pass_copies + [suf_copy] + q_copies + sends1 + sends2 + g_copies:
+    for copy in sends2:
         copy.wait_send()
-    for block, dev in yc_peers:
-        remote(res_out.at[block], back_out.at[block], o_s.at[block], o_r.at[block], dev).wait_send()
-        remote(
-            res_stat.at[block], back_stat.at[block], st_s.at[block], st_r.at[block], dev
-        ).wait_send()
 
 
 def local(

time: 60.8 us -> 60.7 us (level)
  no operation moved by 1% of the time
where the time goes in v6:
time: 60.7 us; the launch traced here: 60.4 us
  Pallas kernels  56.9 us (94%)
  local copies, waits for them, and re-layouts  2.77 us (5%)
  between operations  0.75 us (1%)
    pallas_call x1, Pallas kernels, local(): pl.pallas_call(kernel, out_shape=jax.ShapeDtypeStruct((2, TOK, HEAD), BF1...  56.9 us
    unnamed x13, local copies, waits for them, and re-layouts  1.59 us

profile of v6, /device:TPU:2, one launch (start us, length us, event | category | flops | bytes accessed | tf_op | source)
XLA Modules:
  0.0 60.4 jit_solution(12301136413632712634)
XLA Ops:
  0.6 0.0 copy-start
  0.6 0.0 copy-start.3
  0.7 0.0 copy-start.2
  0.7 0.0 copy-start.1
  0.7 0.0 copy-start.5
  0.7 0.0 copy-start.4
  0.7 1.5 %copy-done = bf16[2,256,8,256]{3,2,1,0:T(8,128)(2,1)S(1)} copy-done((bf16[2,256,8,256]{3,2,1,0:T(8,128)(2,1)S(1)}, bf16[2,256,8,256]{3,2,1,0:T(8,128)(2,1)}, u32[]{:S(2)}) %copy-start) | copy-done | bytes 2097176
  2.2 0.5 constant_dynamic-slice_fusion
  2.8 0.0 copy-done.3
  2.8 0.0 copy-done.2
  2.8 0.0 copy-done.1
  2.9 0.0 copy-done.5
  2.9 0.0 copy-done.4
  2.9 56.9 %layer.1 = bf16[2,128,128]{2,1,0:T(8,128)(2,1)S(1)} custom-call(s32[32]{0:T(128)S(1)} %copy-done.1, s32[32]{0:T(128)S(1)} %copy-done.2, s32[32]{0:T(128)S(1)} %copy-done.3, bf16[128,2048]{1,0:T(8,128)(2,1)} %hidden_hbm.1, f32[1,2048]{1,0:T(1,128)} %bitcast.12, f32[1,2048]{1,0:T(1,128)} %bitcast.13, f32[1,128]{1,0:T(1,128)S(1)} %bitcast.10, ...), custom_call_target="tpu_custom_call" | custom-call | tf_op jit(solution)/shard_map/layer/pallas_call | solution.py:532
  59.8 0.6 %slice_bitcast_fusion = (bf16[128,128]{1,0:T(8,128)(2,1)}, bf16[128,128]{1,0:T(8,128)(2,1)}) fusion(bf16[2,128,128]{2,1,0:T(8,128)(2,1)S(1)} %layer.1), kind=kLoop, calls=%fused_computation | loop fusion | bytes 131072 | tf_op jit(solution)/shard_map/squeeze | solution.py:615
  (1 shorter events, 0.0 us)
Async XLA Ops:
  0.6 1.6 %copy-start = (bf16[2,256,8,256]{3,2,1,0:T(8,128)(2,1)S(1)}, bf16[2,256,8,256]{3,2,1,0:T(8,128)(2,1)}, u32[]{:S(2)}) copy-start(bf16[2,256,8,256]{3,2,1,0:T(8,128)(2,1)} %param.26) | copy-start | bytes 6291460
  0.6 2.2 %copy-start.3 = (s32[32]{0:T(128)S(1)}, s32[32]{0:T(128)}, u32[]{:S(2)}) copy-start(s32[32]{0:T(128)} %lengths_ref.1) | copy-start | bytes 388
  0.7 2.2 %copy-start.2 = (s32[32]{0:T(128)S(1)}, s32[32]{0:T(128)}, u32[]{:S(2)}) copy-start(s32[32]{0:T(128)} %request_prefix_ref.1) | copy-start | bytes 388
  0.7 2.2 %copy-start.1 = (s32[32]{0:T(128)S(1)}, s32[32]{0:T(128)}, u32[]{:S(2)}) copy-start(s32[32]{0:T(128)} %table_ref.1) | copy-start | bytes 388
  0.7 2.2 %copy-start.5 = (f32[128]{0:T(128)S(1)}, f32[128]{0:T(128)}, u32[]{:S(2)}) copy-start(f32[128]{0:T(128)} %param.20) | copy-start | bytes 1540
  0.7 2.2 %copy-start.4 = (f32[128]{0:T(128)S(1)}, f32[128]{0:T(128)}, u32[]{:S(2)}) copy-start(f32[128]{0:T(128)} %param.19) | copy-start | bytes 1540

commit v7 on v6

--- a/solution.py
+++ b/solution.py
@@ -277,16 +277,20 @@
         remote(suf.at[2], suf.at[1], suf_s.at[1], suf_r.at[1], mate).start()
 
     send_queries(3, mine, mate)
-    for n, (block, dev) in enumerate(y_peers):
-        remote(q_all.at[block], q_all.at[block], q_s.at[0], q_r.at[block], dev).wait_recv()
-        send_queries(4 + n, block, mate)
-
     pass_copies = []
-    for b, ref in enumerate((kk, vt)):
+
+    def pass_on(b, ref):
         kv_copies[b].wait_recv()
         copy = remote(ref.at[2 + px], ref.at[2 + px], kx_s.at[b], kx_r.at[b], x_partner)
         copy.start()
         pass_copies.append(copy)
+
+    pass_on(0, kk)
+    for n, (block, dev) in enumerate(y_peers):
+        remote(q_all.at[block], q_all.at[block], q_s.at[0], q_r.at[block], dev).wait_recv()
+        send_queries(4 + n, block, mate)
+
+    pass_on(1, vt)
 
     def attend(core, first, keys):
         return slot_part(
@@ -455,19 +459,22 @@
             gathered.at[block], gathered.at[block], g_s.at[0], g_r.at[block], z_peers[0]
         ).wait_recv()
 
-    for i in (3, 2, 1):
+    for i in (3, 2):
         share(m, at_mp(z_rows[i] * 4 + x))
     for dev in x_peers:
         share(m, dev)
-    for i in (1, 2, 3):
+    for hop in (2, 1, 3, 0):
+        share(m, at_mp(z_rows[1] * 4 + lax.rem(x + hop, 4)))
+    for i in (3, 2):
         arrived(z_rows[i] * 4 + x)
         for dev in x_peers:
             share(z_rows[i] * 4 + x, dev)
+    arrived(z_rows[1] * 4 + x)
     for k in (5, 6, 7):
         loads[k].wait()
     square = jnp.zeros((TOK, HEAD), F32)
     gate, up = None, None
-    for i in range(4):
+    for i in (0, 1, 3, 2):
         for hop in (1, 3, 2):
             arrived(z_rows[i] * 4 + lax.rem(x + hop, 4))
         base = z_rows[i] * 4

time: 60.7 us -> 60.5 us (level)
  no operation moved by 1% of the time
where the time goes in v7:
time: 60.5 us; the launch traced here: 60.4 us
  Pallas kernels  56.9 us (94%)
  local copies, waits for them, and re-layouts  2.77 us (5%)
  between operations  0.75 us (1%)
    pallas_call x1, Pallas kernels, local(): pl.pallas_call(kernel, out_shape=jax.ShapeDtypeStruct((2, TOK, HEAD), BF1...  56.9 us
    unnamed x13, local copies, waits for them, and re-layouts  1.59 us

profile of v7, /device:TPU:2, one launch (start us, length us, event | category | flops | bytes accessed | tf_op | source)
XLA Modules:
  0.0 60.4 jit_solution(3525943453583745289)
XLA Ops:
  0.6 0.0 copy-start
  0.6 0.0 copy-start.3
  0.7 0.0 copy-start.2
  0.7 0.0 copy-start.1
  0.7 0.0 copy-start.5
  0.7 0.0 copy-start.4
  0.7 1.5 %copy-done = bf16[2,256,8,256]{3,2,1,0:T(8,128)(2,1)S(1)} copy-done((bf16[2,256,8,256]{3,2,1,0:T(8,128)(2,1)S(1)}, bf16[2,256,8,256]{3,2,1,0:T(8,128)(2,1)}, u32[]{:S(2)}) %copy-start) | copy-done | bytes 2097176
  2.2 0.5 constant_dynamic-slice_fusion
  2.8 0.0 copy-done.3
  2.8 0.0 copy-done.2
  2.8 0.0 copy-done.1
  2.9 0.0 copy-done.5
  2.9 0.0 copy-done.4
  2.9 56.9 %layer.1 = bf16[2,128,128]{2,1,0:T(8,128)(2,1)S(1)} custom-call(s32[32]{0:T(128)S(1)} %copy-done.1, s32[32]{0:T(128)S(1)} %copy-done.2, s32[32]{0:T(128)S(1)} %copy-done.3, bf16[128,2048]{1,0:T(8,128)(2,1)} %hidden_hbm.1, f32[1,2048]{1,0:T(1,128)} %bitcast.12, f32[1,2048]{1,0:T(1,128)} %bitcast.13, f32[1,128]{1,0:T(1,128)S(1)} %bitcast.10, ...), custom_call_target="tpu_custom_call" | custom-call | tf_op jit(solution)/shard_map/layer/pallas_call | solution.py:539
  59.7 0.6 %slice_bitcast_fusion = (bf16[128,128]{1,0:T(8,128)(2,1)}, bf16[128,128]{1,0:T(8,128)(2,1)}) fusion(bf16[2,128,128]{2,1,0:T(8,128)(2,1)S(1)} %layer.1), kind=kLoop, calls=%fused_computation | loop fusion | bytes 131072 | tf_op jit(solution)/shard_map/squeeze | solution.py:622
  (1 shorter events, 0.0 us)
Async XLA Ops:
  0.6 1.6 %copy-start = (bf16[2,256,8,256]{3,2,1,0:T(8,128)(2,1)S(1)}, bf16[2,256,8,256]{3,2,1,0:T(8,128)(2,1)}, u32[]{:S(2)}) copy-start(bf16[2,256,8,256]{3,2,1,0:T(8,128)(2,1)} %param.26) | copy-start | bytes 6291460
  0.6 2.2 %copy-start.3 = (s32[32]{0:T(128)S(1)}, s32[32]{0:T(128)}, u32[]{:S(2)}) copy-start(s32[32]{0:T(128)} %lengths_ref.1) | copy-start | bytes 388
  0.7 2.2 %copy-start.2 = (s32[32]{0:T(128)S(1)}, s32[32]{0:T(128)}, u32[]{:S(2)}) copy-start(s32[32]{0:T(128)} %request_prefix_ref.1) | copy-start | bytes 388
  0.7 2.2 %copy-start.1 = (s32[32]{0:T(128)S(1)}, s32[32]{0:T(128)}, u32[]{:S(2)}) copy-start(s32[32]{0:T(128)} %table_ref.1) | copy-start | bytes 388
  0.7 2.2 %copy-start.5 = (f32[128]{0:T(128)S(1)}, f32[128]{0:T(128)}, u32[]{:S(2)}) copy-start(f32[128]{0:T(128)} %param.20) | copy-start | bytes 1540
  0.7 2.2 %copy-start.4 = (f32[128]{0:T(128)S(1)}, f32[128]{0:T(128)}, u32[]{:S(2)}) copy-start(f32[128]{0:T(128)} %param.19) | copy-start | bytes 1540
